TPU v7x, 32 devices: a whole 2x2x4 slice. The times are simulated.
32 devices in a mesh: space: 4 (over y, x), mode: 8 (over z, core).
Axes of the slice: x: 2, y: 2, z: 4, core: 2. Of those that a mesh axis runs over, the one named last changes fastest.
Arguments:
- excess_phonon_enthalpy: bfloat16 [768, 32, 128, 128], P('mode', 'space'), may hold values from -0.21972656 to 0.21972656
- thermal_offset: float32 [128, 128, 32], P('space', 'mode'), may hold values from -6 to 6
- state_specific_warmth_scaled: float32 [768], P('mode'), may hold values from 0.5 to 2
- scattering_lifetimes: float32 [768], P('mode'), may hold values from 0.5 to 50
- state_polarization_label: int32 [768], P('mode'), may hold values from 0 to 5
- state_orientation_label: int32 [768], P('mode'), may hold values from 0 to 15
- polarization_propagation_rate: float32 [6], replicated, may hold values from 0.3 to 1
- thermal_conductance_bulk: float32 [128, 128, 32], P('space', 'mode'), may hold values from 0.25 to 1
- substance_label: int32 [128, 128, 32], P('space', 'mode'), may hold values 0 or 1
Outputs:
- final_temperature: float32 [128, 128, 32], P('space', 'mode')
- heat_flux: float32 [3, 128, 128, 32], P(None, 'space', 'mode')
Inputs may be any that keep to these rules, and one draw needn't show every extreme that they name: `substance_label`: 1 marks a pore cell.
All inputs are finite; a program needn't handle non-finite values. No bound on the sum of `substance_label` on one device may be relied on, other than what follows from the above.
Results may differ from a plain program's by a relative error of at most 0.0028.
Values may be sent and summed in bfloat16 or wider, within the bound.
A program may use at most 192 MiB of HBM per device.

v0:
```python
import math

import jax
import jax.numpy as jnp
from jax import lax
from jax.sharding import PartitionSpec as P

M = 768
SWEEPS = 4
OUTER = 2


time_step = 0.25
pore_factor = 0.1
kappa_top = 1.0


def padded_2(cells, sides, width):
    for axis, dim in sides:
        count = lax.axis_size(axis)
        ends = count - 1
        head = lax.slice_in_dim(cells, 0, width, axis=dim)
        tail = lax.slice_in_dim(cells, cells.shape[dim] - width, cells.shape[dim], axis=dim)
        cells = jnp.concatenate(
            [
                lax.ppermute(tail, axis, [(i, (i + 1) % count) for i in range(ends)]),
                cells,
                lax.ppermute(head, axis, [((i + 1) % count, i) for i in range(ends)]),
            ],
            axis=dim,
        )
    return cells


def mode_table(
    state_polarization_label,
    state_orientation_label,
    state_specific_warmth_scaled,
    scattering_lifetimes,
    polarization_propagation_rate,
):
    branches = jnp.arange(polarization_propagation_rate.shape[0], dtype=jnp.int32)
    onehot = (state_polarization_label[:, None] == branches[None, :]).astype(jnp.float32)
    speed = jnp.sum(onehot * polarization_propagation_rate[None, :], axis=1)
    polar = state_orientation_label // 4
    azimuth = state_orientation_label % 4
    cosine = (2 * polar + 1).astype(jnp.float32) * 0.25 - 1.0
    sine = jnp.sqrt(1.0 - cosine * cosine)
    angle = (azimuth.astype(jnp.float32) + 0.5) * (math.pi / 2.0)
    velocity = (speed * sine * jnp.cos(angle), speed * sine * jnp.sin(angle), speed * cosine)
    rates = 1.0 / scattering_lifetimes
    capacity = state_specific_warmth_scaled / float(M)
    return (velocity, rates, capacity)


def upwind(padded, temp_slab, along_x, along_y, along_z, rates, capacity):

    def widen(values):
        return values[:, None, None, None]

    current = padded[:, 1:-1]
    z_before = padded[:, :-2]
    z_after = padded[:, 2:]
    x_padded = jnp.pad(current, ((0, 0), (0, 0), (1, 1), (0, 0)))
    y_padded = jnp.pad(current, ((0, 0), (0, 0), (0, 0), (1, 1)))

    def advect(speed, before, after):
        flow = widen(speed)
        return jnp.maximum(flow, 0.0) * (current - before) + jnp.minimum(flow, 0.0) * (
            after - current
        )

    total_advect = advect(along_x, x_padded[:, :, :-2], x_padded[:, :, 2:])
    total_advect = total_advect + advect(along_y, y_padded[:, :, :, :-2], y_padded[:, :, :, 2:])
    total_advect = total_advect + advect(along_z, z_before, z_after)
    updated = (
        current
        - time_step * total_advect
        + time_step * widen(rates) * (widen(capacity) * temp_slab[None] - current)
    )
    weights = jnp.stack([rates, along_x, along_y, along_z])
    moments = jnp.einsum("km,mzxy->kzxy", weights, updated, precision=lax.Precision.HIGHEST)
    return (updated, moments)


def harmonic(first, second):
    summed = first + second
    positive = summed > 0.0
    return jnp.where(positive, 2.0 * first * second / jnp.where(positive, summed, 1.0), 0.0)


def face_table(kappa_ext):
    center = kappa_ext[1:-1, 1:-1]
    z_padded = jnp.pad(center, ((0, 0), (0, 0), (1, 1)))
    return (
        harmonic(center, kappa_ext[2:, 1:-1]),
        harmonic(kappa_ext[:-2, 1:-1], center),
        harmonic(center, kappa_ext[1:-1, 2:]),
        harmonic(kappa_ext[1:-1, :-2], center),
        harmonic(center, z_padded[:, :, 2:]),
        harmonic(z_padded[:, :, :-2], center),
    )


def crop(values, matrix_height, matrix_breadth):
    top = (values.shape[0] - matrix_height) // 2
    left = (values.shape[1] - matrix_breadth) // 2
    return values[top : top + matrix_height, left : left + matrix_breadth]


def apply_operator(padded, faces, total):
    matrix_height = padded.shape[0] - 2
    matrix_breadth = padded.shape[1] - 2
    cut = [crop(face, matrix_height, matrix_breadth) for face in faces]
    center = padded[1:-1, 1:-1]
    z_padded = jnp.pad(center, ((0, 0), (0, 0), (1, 1)))
    spread = cut[0] * (padded[2:, 1:-1] - center) + cut[1] * (padded[:-2, 1:-1] - center)
    spread = spread + cut[2] * (padded[1:-1, 2:] - center) + cut[3] * (padded[1:-1, :-2] - center)
    spread = (
        spread + cut[4] * (z_padded[:, :, 2:] - center) + cut[5] * (z_padded[:, :, :-2] - center)
    )
    return total * center - spread


def divergence(fluxes):
    z_flux = jnp.pad(fluxes[2][1:-1, 1:-1], ((0, 0), (0, 0), (1, 1)))
    summed = (
        fluxes[0][2:, 1:-1] - fluxes[0][:-2, 1:-1] + (fluxes[1][1:-1, 2:] - fluxes[1][1:-1, :-2])
    )
    summed = summed + (z_flux[:, :, 2:] - z_flux[:, :, :-2])
    return summed * 0.5


def chebyshev(rhs, faces, total, extend, matrix_height, matrix_breadth):
    theta = total + 6.0 * kappa_top
    spread = 6.0 * kappa_top
    sigma = theta / spread
    rho = 1.0 / sigma
    residual = rhs
    direction = rhs / theta
    correction = jnp.zeros((matrix_height, matrix_breadth, rhs.shape[2]), jnp.float32)
    for sweep in range(SWEEPS):
        correction = correction + crop(direction, matrix_height, matrix_breadth)
        if sweep < SWEEPS - 1:
            image = apply_operator(extend(direction), faces, total)
            residual = crop(residual, image.shape[0], image.shape[1]) - image
            rho_next = 1.0 / (2.0 * sigma - rho)
            direction = (
                rho_next * rho * crop(direction, image.shape[0], image.shape[1])
                + 2.0 * rho_next / spread * residual
            )
            rho = rho_next
    return correction


def unchanged(direction):
    return direction


def to_slab(block):
    upright = jnp.transpose(block, (2, 0, 1))
    moved = lax.all_to_all(upright, "space", split_axis=0, concat_axis=1, tiled=True)
    return lax.all_gather(moved, "mode", axis=2, tiled=True)


def kinetic(state, temp_slab, velocity, rates, capacity):
    padded = padded_2(state, (("space", 1),), 1)
    local = padded.shape[0]
    group = math.gcd(local, 8)
    count = local // group
    shaped = padded.reshape((count, group) + padded.shape[1:])
    params = (
        velocity[0].reshape(count, group),
        velocity[1].reshape(count, group),
        velocity[2].reshape(count, group),
        rates.reshape(count, group),
        capacity.reshape(count, group),
    )

    def step(carry, inputs):
        block, along_x, along_y, along_z, rate_part, cap_part = inputs
        updated, moments = upwind(
            block.astype(jnp.float32), temp_slab, along_x, along_y, along_z, rate_part, cap_part
        )
        return (carry + moments, updated.astype(jnp.bfloat16))

    start = jnp.zeros((4,) + state.shape[1:], jnp.float32)
    moments, news = lax.scan(step, start, (shaped,) + params)
    return (news.reshape(state.shape), moments)


def per_device(
    excess_phonon_enthalpy,
    thermal_offset,
    state_specific_warmth_scaled,
    scattering_lifetimes,
    state_polarization_label,
    state_orientation_label,
    polarization_propagation_rate,
    thermal_conductance_bulk,
    substance_label,
):
    velocity, rates, capacity = mode_table(
        state_polarization_label,
        state_orientation_label,
        state_specific_warmth_scaled,
        scattering_lifetimes,
        polarization_propagation_rate,
    )
    total = lax.psum(jnp.sum(capacity * rates), "mode")
    kappa = thermal_conductance_bulk * jnp.where(substance_label == 1, pore_factor, 1.0)
    matrix_height = thermal_offset.shape[0]
    matrix_breadth = thermal_offset.shape[1]
    kappa_ext = padded_2(kappa.astype(jnp.bfloat16), (("space", 0), ("mode", 1)), SWEEPS).astype(
        kappa.dtype
    )
    faces = face_table(kappa_ext)
    spatial_entries = thermal_offset
    state = excess_phonon_enthalpy
    fluxes = None
    for outer in range(OUTER):
        temp_slab = to_slab(spatial_entries)
        state, moments = kinetic(state, temp_slab, velocity, rates, capacity)
        reduced = lax.psum_scatter(moments, "mode", scatter_dimension=3, tiled=True)
        summed = lax.all_to_all(reduced, "space", split_axis=2, concat_axis=1, tiled=True)
        blocks = jnp.transpose(summed, (0, 2, 3, 1))
        fluxes = blocks[1:]
        flux_ext = padded_2(
            fluxes.astype(jnp.bfloat16), (("space", 1), ("mode", 2)), SWEEPS
        ).astype(fluxes.dtype)
        rhs = -divergence(flux_ext)
        correction = chebyshev(rhs, faces, total, unchanged, matrix_height, matrix_breadth)
        spatial_entries = blocks[0] / total + correction
    return (spatial_entries, fluxes)


def solution(mesh):
    placed = (
        P("mode", "space", None, None),
        P("space", "mode", None),
        P("mode"),
        P("mode"),
        P("mode"),
        P("mode"),
        P(),
        P("space", "mode", None),
        P("space", "mode", None),
    )
    return jax.shard_map(
        per_device,
        mesh=mesh,
        in_specs=placed,
        out_specs=(P("space", "mode", None), P(None, "space", "mode", None)),
        check_vma=False,
    )
```

profile of v0, /device:TPU:1, one launch (start us, length us, event | category | flops | bytes accessed | tf_op | source)
XLA Modules:
  0.0 1069.5 jit_solution(18058202985075176916)
XLA Ops:
  7.2 8.3 fusion.191
  15.5 5.6 collective-permute-start
  29.0 127.6 %all-to-all-done = f32[4,1,4096]{2,1,0:T(1,128)S(1)} async-done(((f32[4,1,4096]{2,1,0:T(1,128)}), f32[4,1,4096]{2,1,0:T(1,128)S(1)}, u32[]{:S(2)}, u32[]{:S(2)}) %all-to-all-start) | async-done | bytes 65568 | tf_op jit(solution)/shard_map/all_to_all | solution.py:162
  158.4 16.8 %all_gather.6 = f32[8,128,128]{1,2,0:T(8,128)S(1)} all-gather(f32[8,128,16]{1,2,0:T(8,128)S(1)} %all_to_all.55), channel_id=1, replica_groups=mesh['space'=4,'mode'=8] {'mode'}, dimensions={2}, use_global_device_ids=true | all-gather | bytes 589824 | tf_op jit(solution)/shard_map/all_gather | solution.py:163
  175.5 21.7 %pad_maximum_fusion = bf16[96,10,128,128]{3,2,1,0:T(8,128)(2,1)} fusion(bf16[96,1,128,128]{3,2,1,0:T(8,128)(2,1)} %collective-permute-done.1, bf16[96,8,128,128]{3,2,1,0:T(8,128)(2,1)} %param.13, bf16[96,1,128,128]{3,2,1,0:T(8,128)(2,1)} %collective-permute-done), kind=kLoop, calls=%fused_computation.96 | loop fusion | flops 31457280 | bytes 62914560 | tf_op jit(solution)/shard_map/concatenate | solution.py:24
  197.1 198.7 %while.28 = (s32[]{:T(128)}, f32[4,8,128,128]{3,0,2,1:T(4,128)S(1)}, bf16[12,8,8,128,128]{4,1,3,2,0:T(8,128)(2,1)}, f32[12,8]{1,0:T(8,128)S(1)}, f32[12,8]{1,0:T...) while((s32[]{:T(128)}, ...), condition=%wide.region_2.3_spmd.clone, body=%wide.region_1.2_spmd.clone.sunk | while | flops 77856920 | bytes 49284748 | solution.py:188
  201.4 5.4 bitcast_dynamic-update-slice_fusion.2
  206.8 7.0 select_add_fusion.4
  223.3 7.0 select_add_fusion.4
  239.9 7.0 select_add_fusion.4
  251.1 5.4 bitcast_dynamic-update-slice_fusion.2
  256.5 7.0 select_add_fusion.4
  273.0 7.0 select_add_fusion.4
  289.5 7.0 select_add_fusion.4
  300.7 5.4 bitcast_dynamic-update-slice_fusion.2
  306.1 7.0 select_add_fusion.4
  322.6 7.0 select_add_fusion.4
  339.1 7.0 select_add_fusion.4
  355.7 7.0 select_add_fusion.4
  372.2 7.0 select_add_fusion.4
  383.4 5.4 bitcast_dynamic-update-slice_fusion.2
  388.8 7.0 select_add_fusion.4
  398.7 14.7 %copy.66 = bf16[12,8,8,128,128]{4,3,2,1,0:T(8,128)(2,1)S(1)} copy(bf16[12,8,8,128,128]{4,1,3,2,0:T(8,128)(2,1)} %get-tuple-element.241) | data formatting | bytes 50331648 | tf_op jit(solution)/shard_map/while | solution.py:188
  440.6 50.4 %collective-permute-done.8 = bf16[4,16,32]{0,1,2:T(8,128)(2,1)S(1)} collective-permute-done((bf16[4,16,32]{0,1,2:T(8,128)(2,1)S(1)}, bf16[4,16,32]{0,1,2:T(8,128)(2,1)S(1)}, u32[]{:S(2)}, u32[]{:S(2)}) %collective-permute-start.8) | collective-permute-done | bytes 4128 | tf_op jit(solution)/shard_map/ppermute | solution.py:26
  491.0 71.8 %collective-permute-done.9 = bf16[4,16,32]{0,1,2:T(8,128)(2,1)S(1)} collective-permute-done((bf16[4,16,32]{0,1,2:T(8,128)(2,1)S(1)}, bf16[4,16,32]{0,1,2:T(8,128)(2,1)S(1)}, u32[]{:S(2)}, u32[]{:S(2)}) %collective-permute-start.9) | collective-permute-done | bytes 4128 | tf_op jit(solution)/shard_map/ppermute | solution.py:28
  569.5 14.2 %psum.7 = f32[]{:T(128)} all-reduce(f32[]{:T(128)} %get-tuple-element.450), channel_id=1, replica_groups=mesh['space'=4,'mode'=8] {'mode'}, use_global_device_ids=true, to_apply=%region_5.6 | all-reduce | flops 1 | bytes 8 | tf_op jit(solution)/shard_map/psum | solution.py:210
  597.2 9.5 collective-permute-done.5
  613.8 6.0 copy.67
  619.8 6.0 copy.68
  638.9 21.7 %pad_maximum_fusion.1 = bf16[12,8,10,128,128]{4,1,3,2,0:T(8,128)(2,1)} fusion(bf16[12,8,1,128,128]{4,1,3,2,0:T(8,128)(2,1)} %copy.68, bf16[12,8,8,128,128]{4,1,3,2,0:T(8,128)(2,1)} %get-tuple-element.241, bf16[12,8,1,128,128]{4,1,3,2,0:T(8,128)(2,1)} %copy.67), kind=kLoop, calls=%fused_computation.97 | loop fusion | flops 31457280 | bytes 62914560 | tf_op jit(solution)/shard_map/concatenate | solution.py:24
  661.9 14.8 %all_gather.7 = f32[8,128,128]{1,2,0:T(8,128)S(1)} all-gather(f32[8,128,16]{1,2,0:T(8,128)S(1)} %all_to_all.63), channel_id=1, replica_groups=mesh['space'=4,'mode'=8] {'mode'}, dimensions={2}, use_global_device_ids=true | all-gather | bytes 589824 | tf_op jit(solution)/shard_map/all_gather | solution.py:163
  676.9 284.5 %while.29 = (s32[]{:T(128)}, f32[4,8,128,128]{3,0,2,1:T(4,128)}, f32[12,8]{1,0:T(8,128)}, f32[12,8]{1,0:T(8,128)S(1)}, f32[12,8]{1,0:T(8,128)S(1)}, /*index=5*/f...) while((s32[]{:T(128)}, f32[4,8,128,128]{3,0,2,1:T(4,128)}, ...), condition=%wide.region_7.8_spmd.clone, body=%wide.region_6.7_spmd.clone.sunk | while | flops 76808344 | bytes 54527136 | solution.py:188
  684.1 16.5 %select_add_fusion.5 = f32[4,8,128,128]{3,0,2,1:T(4,128)} fusion(f32[4,8,128,128]{3,0,2,1:T(4,128)} %get-tuple-element.694, f32[8,8,128,128]{3,0,2,1:T(8,128)} %slice.1346, f32[8,10,128,128]{3,0,2,1:T(8,128)} %copy-done, f32[8,128,128]{2,1,0:T(8,128)S(1)} %get-tuple-element.712, f32[8]{0:T(128)S(1)} %fusion.206, f32[8]{0:T(128)S(1)} %get-tuple-element.638, ...), kind=kOutput, calls=%fused_computation.62.clone.1 | convolution fusion | flops 75497568 | bytes 17301888 | tf_op jit(solution)/shard_map/while/body/eval_jaxpr/km,mzxy->kzxy/dot_general | solution.py:82
  707.8 16.5 %select_add_fusion.5 = f32[4,8,128,128]{3,0,2,1:T(4,128)} fusion(f32[4,8,128,128]{3,0,2,1:T(4,128)} %get-tuple-element.694, f32[8,8,128,128]{3,0,2,1:T(8,128)} %slice.1346, f32[8,10,128,128]{3,0,2,1:T(8,128)} %copy-done, f32[8,128,128]{2,1,0:T(8,128)S(1)} %get-tuple-element.712, f32[8]{0:T(128)S(1)} %fusion.206, f32[8]{0:T(128)S(1)} %get-tuple-element.638, ...), kind=kOutput, calls=%fused_computation.62.clone.1 | convolution fusion | flops 75497568 | bytes 17301888 | tf_op jit(solution)/shard_map/while/body/eval_jaxpr/km,mzxy->kzxy/dot_general | solution.py:82
  731.5 16.5 %select_add_fusion.5 = f32[4,8,128,128]{3,0,2,1:T(4,128)} fusion(f32[4,8,128,128]{3,0,2,1:T(4,128)} %get-tuple-element.694, f32[8,8,128,128]{3,0,2,1:T(8,128)} %slice.1346, f32[8,10,128,128]{3,0,2,1:T(8,128)} %copy-done, f32[8,128,128]{2,1,0:T(8,128)S(1)} %get-tuple-element.712, f32[8]{0:T(128)S(1)} %fusion.206, f32[8]{0:T(128)S(1)} %get-tuple-element.638, ...), kind=kOutput, calls=%fused_computation.62.clone.1 | convolution fusion | flops 75497568 | bytes 17301888 | tf_op jit(solution)/shard_map/while/body/eval_jaxpr/km,mzxy->kzxy/dot_general | solution.py:82
  755.2 16.5 %select_add_fusion.5 = f32[4,8,128,128]{3,0,2,1:T(4,128)} fusion(f32[4,8,128,128]{3,0,2,1:T(4,128)} %get-tuple-element.694, f32[8,8,128,128]{3,0,2,1:T(8,128)} %slice.1346, f32[8,10,128,128]{3,0,2,1:T(8,128)} %copy-done, f32[8,128,128]{2,1,0:T(8,128)S(1)} %get-tuple-element.712, f32[8]{0:T(128)S(1)} %fusion.206, f32[8]{0:T(128)S(1)} %get-tuple-element.638, ...), kind=kOutput, calls=%fused_computation.62.clone.1 | convolution fusion | flops 75497568 | bytes 17301888 | tf_op jit(solution)/shard_map/while/body/eval_jaxpr/km,mzxy->kzxy/dot_general | solution.py:82
  778.9 16.5 %select_add_fusion.5 = f32[4,8,128,128]{3,0,2,1:T(4,128)} fusion(f32[4,8,128,128]{3,0,2,1:T(4,128)} %get-tuple-element.694, f32[8,8,128,128]{3,0,2,1:T(8,128)} %slice.1346, f32[8,10,128,128]{3,0,2,1:T(8,128)} %copy-done, f32[8,128,128]{2,1,0:T(8,128)S(1)} %get-tuple-element.712, f32[8]{0:T(128)S(1)} %fusion.206, f32[8]{0:T(128)S(1)} %get-tuple-element.638, ...), kind=kOutput, calls=%fused_computation.62.clone.1 | convolution fusion | flops 75497568 | bytes 17301888 | tf_op jit(solution)/shard_map/while/body/eval_jaxpr/km,mzxy->kzxy/dot_general | solution.py:82
  802.6 16.5 %select_add_fusion.5 = f32[4,8,128,128]{3,0,2,1:T(4,128)} fusion(f32[4,8,128,128]{3,0,2,1:T(4,128)} %get-tuple-element.694, f32[8,8,128,128]{3,0,2,1:T(8,128)} %slice.1346, f32[8,10,128,128]{3,0,2,1:T(8,128)} %copy-done, f32[8,128,128]{2,1,0:T(8,128)S(1)} %get-tuple-element.712, f32[8]{0:T(128)S(1)} %fusion.206, f32[8]{0:T(128)S(1)} %get-tuple-element.638, ...), kind=kOutput, calls=%fused_computation.62.clone.1 | convolution fusion | flops 75497568 | bytes 17301888 | tf_op jit(solution)/shard_map/while/body/eval_jaxpr/km,mzxy->kzxy/dot_general | solution.py:82
  826.3 16.5 %select_add_fusion.5 = f32[4,8,128,128]{3,0,2,1:T(4,128)} fusion(f32[4,8,128,128]{3,0,2,1:T(4,128)} %get-tuple-element.694, f32[8,8,128,128]{3,0,2,1:T(8,128)} %slice.1346, f32[8,10,128,128]{3,0,2,1:T(8,128)} %copy-done, f32[8,128,128]{2,1,0:T(8,128)S(1)} %get-tuple-element.712, f32[8]{0:T(128)S(1)} %fusion.206, f32[8]{0:T(128)S(1)} %get-tuple-element.638, ...), kind=kOutput, calls=%fused_computation.62.clone.1 | convolution fusion | flops 75497568 | bytes 17301888 | tf_op jit(solution)/shard_map/while/body/eval_jaxpr/km,mzxy->kzxy/dot_general | solution.py:82
  850.0 16.5 %select_add_fusion.5 = f32[4,8,128,128]{3,0,2,1:T(4,128)} fusion(f32[4,8,128,128]{3,0,2,1:T(4,128)} %get-tuple-element.694, f32[8,8,128,128]{3,0,2,1:T(8,128)} %slice.1346, f32[8,10,128,128]{3,0,2,1:T(8,128)} %copy-done, f32[8,128,128]{2,1,0:T(8,128)S(1)} %get-tuple-element.712, f32[8]{0:T(128)S(1)} %fusion.206, f32[8]{0:T(128)S(1)} %get-tuple-element.638, ...), kind=kOutput, calls=%fused_computation.62.clone.1 | convolution fusion | flops 75497568 | bytes 17301888 | tf_op jit(solution)/shard_map/while/body/eval_jaxpr/km,mzxy->kzxy/dot_general | solution.py:82
  873.7 16.5 %select_add_fusion.5 = f32[4,8,128,128]{3,0,2,1:T(4,128)} fusion(f32[4,8,128,128]{3,0,2,1:T(4,128)} %get-tuple-element.694, f32[8,8,128,128]{3,0,2,1:T(8,128)} %slice.1346, f32[8,10,128,128]{3,0,2,1:T(8,128)} %copy-done, f32[8,128,128]{2,1,0:T(8,128)S(1)} %get-tuple-element.712, f32[8]{0:T(128)S(1)} %fusion.206, f32[8]{0:T(128)S(1)} %get-tuple-element.638, ...), kind=kOutput, calls=%fused_computation.62.clone.1 | convolution fusion | flops 75497568 | bytes 17301888 | tf_op jit(solution)/shard_map/while/body/eval_jaxpr/km,mzxy->kzxy/dot_general | solution.py:82
  897.5 16.5 %select_add_fusion.5 = f32[4,8,128,128]{3,0,2,1:T(4,128)} fusion(f32[4,8,128,128]{3,0,2,1:T(4,128)} %get-tuple-element.694, f32[8,8,128,128]{3,0,2,1:T(8,128)} %slice.1346, f32[8,10,128,128]{3,0,2,1:T(8,128)} %copy-done, f32[8,128,128]{2,1,0:T(8,128)S(1)} %get-tuple-element.712, f32[8]{0:T(128)S(1)} %fusion.206, f32[8]{0:T(128)S(1)} %get-tuple-element.638, ...), kind=kOutput, calls=%fused_computation.62.clone.1 | convolution fusion | flops 75497568 | bytes 17301888 | tf_op jit(solution)/shard_map/while/body/eval_jaxpr/km,mzxy->kzxy/dot_general | solution.py:82
  921.2 16.5 %select_add_fusion.5 = f32[4,8,128,128]{3,0,2,1:T(4,128)} fusion(f32[4,8,128,128]{3,0,2,1:T(4,128)} %get-tuple-element.694, f32[8,8,128,128]{3,0,2,1:T(8,128)} %slice.1346, f32[8,10,128,128]{3,0,2,1:T(8,128)} %copy-done, f32[8,128,128]{2,1,0:T(8,128)S(1)} %get-tuple-element.712, f32[8]{0:T(128)S(1)} %fusion.206, f32[8]{0:T(128)S(1)} %get-tuple-element.638, ...), kind=kOutput, calls=%fused_computation.62.clone.1 | convolution fusion | flops 75497568 | bytes 17301888 | tf_op jit(solution)/shard_map/while/body/eval_jaxpr/km,mzxy->kzxy/dot_general | solution.py:82
  944.9 16.5 %select_add_fusion.5 = f32[4,8,128,128]{3,0,2,1:T(4,128)} fusion(f32[4,8,128,128]{3,0,2,1:T(4,128)} %get-tuple-element.694, f32[8,8,128,128]{3,0,2,1:T(8,128)} %slice.1346, f32[8,10,128,128]{3,0,2,1:T(8,128)} %copy-done, f32[8,128,128]{2,1,0:T(8,128)S(1)} %get-tuple-element.712, f32[8]{0:T(128)S(1)} %fusion.206, f32[8]{0:T(128)S(1)} %get-tuple-element.638, ...), kind=kOutput, calls=%fused_computation.62.clone.1 | convolution fusion | flops 75497568 | bytes 17301888 | tf_op jit(solution)/shard_map/while/body/eval_jaxpr/km,mzxy->kzxy/dot_general | solution.py:82
  965.9 33.2 %reduce-scatter.5.cloned.1.call-done = f32[4,8,128,16]{2,1,0,3:T(8,128)} async-done(((f32[4,8,128,128]{2,1,0,3:T(8,128)}), f32[4,8,128,16]{2,1,0,3:T(8,128)}) %reduce-scatter.5.cloned.1.call-update) | async-done | bytes 262160 | tf_op jit(solution)/shard_map/reduce_scatter | solution.py:224
  1005.9 7.7 all_to_all.72
  1029.6 8.9 collective-permute-done.13
  1039.6 6.3 collective-permute-start.14
  (379 shorter events, 303.3 us)
Async XLA Ops:
  7.2 15.2 %copy-start.4 = (f32[32,16,32]{2,1,0:T(8,128)S(1)}, f32[32,16,32]{2,1,0:T(8,128)}, u32[]{:S(2)}) copy-start(f32[32,16,32]{2,1,0:T(8,128)} %param.14) | copy-start | bytes 196612
  7.2 20.5 %copy-start.14 = (s32[96]{0:T(128)S(1)}, s32[96]{0:T(128)}, u32[]{:S(2)}) copy-start(s32[96]{0:T(128)} %param.17) | copy-start | bytes 1156
  7.2 20.5 %copy-start.13 = (f32[6]{0:T(128)S(1)}, f32[6]{0:T(128)}, u32[]{:S(2)}) copy-start(f32[6]{0:T(128)} %param.19) | copy-start | bytes 76
  7.2 20.6 %copy-start.10 = (s32[96]{0:T(128)S(1)}, s32[96]{0:T(128)}, u32[]{:S(2)}) copy-start(s32[96]{0:T(128)} %param.18) | copy-start | bytes 1156
  7.2 20.7 %copy-start.11 = (f32[96]{0:T(128)S(1)}, f32[96]{0:T(128)}, u32[]{:S(2)}) copy-start(f32[96]{0:T(128)} %param.15) | copy-start | bytes 1156
  7.2 20.7 %copy-start.12 = (f32[96]{0:T(128)S(1)}, f32[96]{0:T(128)}, u32[]{:S(2)}) copy-start(f32[96]{0:T(128)} %param.16) | copy-start | bytes 1156
  15.5 159.9 %collective-permute-start = (bf16[96,1,128,128]{3,2,1,0:T(8,128)(2,1)}, bf16[96,1,128,128]{3,2,1,0:T(8,128)(2,1)}, u32[]{:S(2)}, u32[]{:S(2)}) collective-permute-start(bf16[96,1,128,128]{3,2,1,0:T(8,128)(2,1)} %get-tuple-element.466), channel_id=1, source_target_pairs={{0,8},{8,16},{16,24},{1,9},{9,17},{17,25},{2,10},{10,18},{18,26},{... | collective-permute-start | bytes 9437192 | tf_op jit(solution)/shard_map/ppermute | solution.py:26
  21.1 154.4 %collective-permute-start.1 = (bf16[96,1,128,128]{3,2,1,0:T(8,128)(2,1)}, bf16[96,1,128,128]{3,2,1,0:T(8,128)(2,1)}, u32[]{:S(2)}, u32[]{:S(2)}) collective-permute-start(bf16[96,1,128,128]{3,2,1,0:T(8,128)(2,1)} %get-tuple-element.467), channel_id=1, source_target_pairs={{8,0},{16,8},{24,16},{9,1},{17,9},{25,17},{10,2},{18,10},{26,18},{... | collective-permute-start | bytes 9437192 | tf_op jit(solution)/shard_map/ppermute | solution.py:28
  23.4 133.2 %all-to-all-start = ((f32[4,1,4096]{2,1,0:T(1,128)}), f32[4,1,4096]{2,1,0:T(1,128)S(1)}, u32[]{:S(2)}, u32[]{:S(2)}) async-start(f32[4,1,4096]{2,1,0:T(1,128)} %reshape.240), calls=%async_computation | async-start | bytes 131072 | tf_op jit(solution)/shard_map/all_to_all | solution.py:162
  27.7 404.0 %reduce-scatter.3.cloned.1.call-start = ((), (), s32[]{:S(2)}) async-start(), calls=%async_computation.6 | async-start | bytes 2359296 | tf_op jit(solution)/shard_map/reduce_scatter | solution.py:224
  395.8 17.7 %copy-start.7 = (f32[12,8]{1,0:T(8,128)}, f32[12,8]{1,0:T(8,128)S(1)}, u32[]{:S(2)}) copy-start(f32[12,8]{1,0:T(8,128)S(1)} %get-tuple-element.750) | copy-start | bytes 1156
  395.8 17.7 %copy-start.8 = (f32[12,8]{1,0:T(8,128)}, f32[12,8]{1,0:T(8,128)S(1)}, u32[]{:S(2)}) copy-start(f32[12,8]{1,0:T(8,128)S(1)} %get-tuple-element.751) | copy-start | bytes 1156
  395.8 17.7 %copy-start.9 = (f32[12,8]{1,0:T(8,128)}, f32[12,8]{1,0:T(8,128)S(1)}, u32[]{:S(2)}) copy-start(f32[12,8]{1,0:T(8,128)S(1)} %get-tuple-element.752) | copy-start | bytes 1156
  413.5 10.1 copy-start.5
  413.5 10.3 copy-start.6
  417.6 196.2 %collective-permute-start.2 = (bf16[96,1,128,128]{3,2,1,0:T(8,128)(2,1)}, bf16[96,1,128,128]{3,2,1,0:T(8,128)(2,1)}, u32[]{:S(2)}, u32[]{:S(2)}) collective-permute-start(bf16[96,1,128,128]{3,2,1,0:T(8,128)(2,1)} %get-tuple-element.464), channel_id=1, source_target_pairs={{0,8},{8,16},{16,24},{1,9},{9,17},{17,25},{2,10},{10,18},{18,26},{... | collective-permute-start | bytes 9437192 | tf_op jit(solution)/shard_map/ppermute | solution.py:26
  422.3 197.5 %collective-permute-start.3 = (bf16[96,1,128,128]{3,2,1,0:T(8,128)(2,1)}, bf16[96,1,128,128]{3,2,1,0:T(8,128)(2,1)}, u32[]{:S(2)}, u32[]{:S(2)}) collective-permute-start(bf16[96,1,128,128]{3,2,1,0:T(8,128)(2,1)} %get-tuple-element.465), channel_id=1, source_target_pairs={{8,0},{16,8},{24,16},{9,1},{17,9},{25,17},{10,2},{18,10},{26,18},{... | collective-permute-start | bytes 9437192 | tf_op jit(solution)/shard_map/ppermute | solution.py:28
  424.2 66.8 %collective-permute-start.8 = (bf16[4,16,32]{0,1,2:T(8,128)(2,1)S(1)}, bf16[4,16,32]{0,1,2:T(8,128)(2,1)S(1)}, u32[]{:S(2)}, u32[]{:S(2)}) collective-permute-start(bf16[4,16,32]{0,1,2:T(8,128)(2,1)S(1)} %get-tuple-element.491), channel_id=1, source_target_pairs={{0,8},{8,16},{16,24},{1,9},{9,17},{17,25},{2,10},{10,18},{18,26},{... | collective-permute-start | bytes 12296 | tf_op jit(solution)/shard_map/ppermute | solution.py:26
  428.2 134.6 %collective-permute-start.9 = (bf16[4,16,32]{0,1,2:T(8,128)(2,1)S(1)}, bf16[4,16,32]{0,1,2:T(8,128)(2,1)S(1)}, u32[]{:S(2)}, u32[]{:S(2)}) collective-permute-start(bf16[4,16,32]{0,1,2:T(8,128)(2,1)S(1)} %get-tuple-element.492), channel_id=1, source_target_pairs={{8,0},{16,8},{24,16},{9,1},{17,9},{25,17},{10,2},{18,10},{26,18},{... | collective-permute-start | bytes 12296 | tf_op jit(solution)/shard_map/ppermute | solution.py:28
  437.2 147.7 %all-to-all-start.1 = ((f32[4,1,16384]{2,1,0:T(1,128)}), f32[4,1,16384]{2,1,0:T(1,128)S(1)}, u32[]{:S(2)}, u32[]{:S(2)}) async-start(f32[4,1,16384]{2,1,0:T(1,128)} %reshape.242), calls=%async_computation.2 | async-start | bytes 524288 | tf_op jit(solution)/shard_map/all_to_all | solution.py:225
  563.0 21.6 %collective-permute-start.10 = (bf16[40,4,32]{0,1,2:T(4,128)(2,1)S(1)}, bf16[40,4,32]{0,1,2:T(4,128)(2,1)S(1)}, u32[]{:S(2)}, u32[]{:S(2)}) collective-permute-start(bf16[40,4,32]{0,1,2:T(4,128)(2,1)S(1)} %get-tuple-element.489), channel_id=1, source_target_pairs={{0,1},{1,2},{2,3},{3,4},{4,5},{5,6},{6,7},{8,9},{9,10},{10,11},{11... | collective-permute-start | bytes 30728 | tf_op jit(solution)/shard_map/ppermute | solution.py:26
  567.6 17.0 %collective-permute-start.11 = (bf16[40,4,32]{0,1,2:T(4,128)(2,1)S(1)}, bf16[40,4,32]{0,1,2:T(4,128)(2,1)S(1)}, u32[]{:S(2)}, u32[]{:S(2)}) collective-permute-start(bf16[40,4,32]{0,1,2:T(4,128)(2,1)S(1)} %get-tuple-element.490), channel_id=1, source_target_pairs={{1,0},{2,1},{3,2},{4,3},{5,4},{6,5},{7,6},{9,8},{10,9},{11,10},{12... | collective-permute-start | bytes 30728 | tf_op jit(solution)/shard_map/ppermute | solution.py:28
  589.1 8.1 collective-permute-start.4
  591.3 15.4 %collective-permute-start.5 = (bf16[3,4,16,32]{1,2,3,0:T(8,128)(2,1)S(1)}, bf16[3,4,16,32]{1,2,3,0:T(8,128)(2,1)S(1)}, u32[]{:S(2)}, u32[]{:S(2)}) collective-permute-start(bf16[3,4,16,32]{1,2,3,0:T(8,128)(2,1)S(1)} %get-tuple-element.479), channel_id=1, source_target_pairs={{8,0},{16,8},{24,16},{9,1},{17,9},{25,17},{10,2},{18,10},{26,18},{... | collective-permute-start | bytes 36872 | tf_op jit(solution)/shard_map/ppermute | solution.py:28
  607.1 18.7 %collective-permute-start.6 = (bf16[3,40,4,32]{1,2,3,0:T(4,128)(2,1)S(1)}, bf16[3,40,4,32]{1,2,3,0:T(4,128)(2,1)S(1)}, u32[]{:S(2)}, u32[]{:S(2)}) collective-permute-start(bf16[3,40,4,32]{1,2,3,0:T(4,128)(2,1)S(1)} %get-tuple-element.476), channel_id=1, source_target_pairs={{0,1},{1,2},{2,3},{3,4},{4,5},{5,6},{6,7},{8,9},{9,10},{10,11},{11... | collective-permute-start | bytes 92168 | tf_op jit(solution)/shard_map/ppermute | solution.py:26
  609.7 16.2 %collective-permute-start.7 = (bf16[3,40,4,32]{1,2,3,0:T(4,128)(2,1)S(1)}, bf16[3,40,4,32]{1,2,3,0:T(4,128)(2,1)S(1)}, u32[]{:S(2)}, u32[]{:S(2)}) collective-permute-start(bf16[3,40,4,32]{1,2,3,0:T(4,128)(2,1)S(1)} %get-tuple-element.477), channel_id=1, source_target_pairs={{1,0},{2,1},{3,2},{4,3},{5,4},{6,5},{7,6},{9,8},{10,9},{11,10},{12... | collective-permute-start | bytes 92168 | tf_op jit(solution)/shard_map/ppermute | solution.py:28
  635.6 25.1 %all-to-all-start.2 = ((f32[4,1,4096]{2,1,0:T(1,128)}), f32[4,1,4096]{2,1,0:T(1,128)S(1)}, u32[]{:S(2)}, u32[]{:S(2)}) async-start(f32[4,1,4096]{2,1,0:T(1,128)} %reshape.244), calls=%async_computation.3 | async-start | bytes 131072 | tf_op jit(solution)/shard_map/all_to_all | solution.py:162
  638.9 360.2 %reduce-scatter.5.cloned.1.call-start = ((), (), s32[]{:S(2)}) async-start(), calls=%async_computation.7 | async-start | bytes 2359296 | tf_op jit(solution)/shard_map/reduce_scatter | solution.py:224
  679.8 3.6 copy-start
  703.5 3.6 copy-start
  727.2 3.6 copy-start
  750.9 3.6 copy-start
  774.6 3.6 copy-start
  798.3 3.6 copy-start
  822.1 3.6 copy-start
  845.8 3.6 copy-start
  869.5 3.6 copy-start
  893.2 3.6 copy-start
  916.9 3.6 copy-start
  940.6 3.6 copy-start
  1020.9 28.6 %copy-start.1 = (f32[4,4,8,32,16]{3,4,2,1,0:T(8,128)S(1)}, f32[4,4,8,32,16]{3,4,2,1,0:T(8,128)}, u32[]{:S(2)}) copy-start(f32[4,4,8,32,16]{3,4,2,1,0:T(8,128)} %copy.80) | copy-start | bytes 786436
  1022.3 7.3 collective-permute-start.12
  1024.9 13.6 %collective-permute-start.13 = (bf16[3,4,16,32]{1,2,3,0:T(8,128)(2,1)S(1)}, bf16[3,4,16,32]{1,2,3,0:T(8,128)(2,1)S(1)}, u32[]{:S(2)}, u32[]{:S(2)}) collective-permute-start(bf16[3,4,16,32]{1,2,3,0:T(8,128)(2,1)S(1)} %get-tuple-element.481), channel_id=1, source_target_pairs={{8,0},{16,8},{24,16},{9,1},{17,9},{25,17},{10,2},{18,10},{26,18},{... | collective-permute-start | bytes 36872 | tf_op jit(solution)/shard_map/ppermute | solution.py:28
  1029.6 16.4 %copy-start.2 = (bf16[3,4,16,32]{1,2,3,0:T(8,128)(2,1)}, bf16[3,4,16,32]{1,2,3,0:T(8,128)(2,1)S(1)}, u32[]{:S(2)}) copy-start(bf16[3,4,16,32]{1,2,3,0:T(8,128)(2,1)S(1)} %collective-permute-done.12) | copy-start | bytes 36868
  1038.5 11.0 %copy-start.3 = (bf16[3,4,16,32]{1,2,3,0:T(8,128)(2,1)}, bf16[3,4,16,32]{1,2,3,0:T(8,128)(2,1)S(1)}, u32[]{:S(2)}) copy-start(bf16[3,4,16,32]{1,2,3,0:T(8,128)(2,1)S(1)} %collective-permute-done.13) | copy-start | bytes 36868
  1039.6 11.3 %collective-permute-start.14 = (bf16[3,40,4,32]{1,2,3,0:T(4,128)(2,1)}, bf16[3,40,4,32]{1,2,3,0:T(4,128)(2,1)}, u32[]{:S(2)}, u32[]{:S(2)}) collective-permute-start(bf16[3,40,4,32]{1,2,3,0:T(4,128)(2,1)} %get-tuple-element.471), channel_id=1, source_target_pairs={{0,1},{1,2},{2,3},{3,4},{4,5},{5,6},{6,7},{8,9},{9,10},{10,11},{11... | collective-permute-start | bytes 92168 | tf_op jit(solution)/shard_map/ppermute | solution.py:26
  1046.0 6.3 collective-permute-start.15
Sparse Core Ops, SparseCore 0:
  398.9 32.7 reduce-scatter.2
  966.0 32.9 reduce-scatter.4
where the time goes:
time: 1080 us; the launch traced here: 1070 us
  waiting for transfers between devices  312 us (29%)
  matrix products  282 us (26%)
  other arithmetic  187 us (17%)
  local copies, waits for them, and re-layouts  157 us (15%)
  starting transfers between devices  59.3 us (5%)
  blocking collectives  53.6 us (5%)
  between operations  15.7 us (1%)
    dot_general x24, matrix products, upwind(): jnp.einsum('km,mzxy->kzxy', weights, updated, precision=lax.Precision.HIG...  282 us
    all_to_all x2, waiting for transfers between devices, to_slab(): lax.all_to_all(upright, 'space', split_axis=0, concat_axis=1, tiled=True)  128 us
    ppermute x8, waiting for transfers between devices, padded_2(): lax.ppermute(head, axis, [((i + 1) % count, i) for i in range(ends)])  91.5 us
    dynamic_update_slice x12, other arithmetic, kinetic(): moments, news = lax.scan(step, start, (shaped,) + params)  64.1 us
    ppermute x8, waiting for transfers between devices, padded_2(): lax.ppermute(tail, axis, [(i, (i + 1) % count) for i in range(ends)])  57.9 us
    convert_element_type x24, other arithmetic, step(): block.astype(jnp.float32)  47.1 us
    concatenate x2, other arithmetic, padded_2(): jnp.concatenate([lax.ppermute(tail, axis, [(i, (i + 1) % count) for i in...  43.4 us
    reduce_scatter x2, waiting for transfers between devices, per_device(): reduced = lax.psum_scatter(moments, 'mode', scatter_dimension=3, tiled=True)  35.4 us
  transfers between devices with their start and end apart: 21, of which 10 were waited for; matrix products, arithmetic and copies ran while one was open for 7% of the time, Pallas kernels for 0%

commit v1 on v0

v1 whole, which is shorter than its diff:
```python
import functools
import math

import jax
import jax.numpy as jnp
from jax import lax
from jax.experimental import pallas as pl
from jax.experimental.pallas import tpu as pltpu
from jax.sharding import PartitionSpec as P

SWEEPS = 4
HALO = 2 * SWEEPS
time_step = 0.25
pore_factor = 0.1
kappa_top = 1.0

UNIT = ((1, 0, 0), (-1, 0, 0), (0, 1, 0), (0, -1, 0), (0, 0, 1), (0, 0, -1))
ONE = ((0, 0, 0),) + UNIT
PAIRS = tuple(
    (i, j)
    for i in range(6)
    for j in range(i, 6)
    if i // 2 != j // 2 or i == j
)
TWO = tuple(tuple(UNIT[i][a] + UNIT[j][a] for a in range(3)) for i, j in PAIRS)
OFFSETS = ONE + TWO


def mode_table(labels, orientation, warmth, lifetimes, rate_of, modes):
    branches = jnp.arange(rate_of.shape[0], dtype=jnp.int32)
    onehot = (labels[:, None] == branches[None, :]).astype(jnp.float32)
    speed = jnp.sum(onehot * rate_of[None, :], axis=1)
    polar = orientation // 4
    azimuth = orientation % 4
    cosine = (2 * polar + 1).astype(jnp.float32) * 0.25 - 1.0
    sine = jnp.sqrt(1.0 - cosine * cosine)
    angle = (azimuth.astype(jnp.float32) + 0.5) * (math.pi / 2.0)
    velocity = (speed * sine * jnp.cos(angle), speed * sine * jnp.sin(angle), speed * cosine)
    return velocity, 1.0 / lifetimes, warmth / float(modes)


def stencils(velocity, rates):
    push = []
    for v in velocity:
        push.append(time_step * jnp.maximum(v, 0.0))
        push.append(time_step * jnp.maximum(-v, 0.0))
    center = 1.0 - sum(push) - time_step * rates
    once = [center] + push
    twice = [center * center] + [2.0 * center * p for p in push]
    for i, j in PAIRS:
        twice.append((1.0 if i == j else 2.0) * push[i] * push[j])
    return jnp.stack(once), jnp.stack(twice)


def moments_kernel(e_ref, a_ref, out_ref, mid, plus, minus):
    z = pl.program_id(0)
    xb = pl.program_id(1)
    width = e_ref.shape[2]
    lanes = e_ref.shape[3]
    planes = mid.shape[0]
    across = mid.shape[1] - 4

    @pl.when((z == 0) & (xb == 0))
    def _():
        def clear(p, _):
            for ref in (mid, plus, minus):
                ref[p] = jnp.zeros(ref.shape[1:], jnp.float32)
            return 0

        lax.fori_loop(0, planes, clear, 0)

    lane = lax.broadcasted_iota(jnp.int32, (8, lanes), 1)
    turned = jnp.transpose(e_ref[:, 0], (1, 0, 2))
    a = a_ref[...]
    for i in range(0, width, 2):
        pair = jnp.concatenate([turned[i], turned[i + 1]], axis=1)
        fields = jnp.dot(
            a, jnp.concatenate([pair, pair], axis=0), preferred_element_type=jnp.float32
        )
        for j in range(2):
            x = xb * width + (i + j)
            for n, (dx, dy, dz) in enumerate(OFFSETS):
                part = fields[8 * n : 8 * n + 8, lanes * j : lanes * (j + 1)]
                if dy == 2:
                    part = jnp.where(lane >= 2, pltpu.roll(part, 2, 1), 0.0)
                elif dy == -2:
                    part = jnp.where(lane < lanes - 2, pltpu.roll(part, lanes - 2, 1), 0.0)
                ref = {1: plus, -1: minus}.get(dy, mid)
                ref[z + (2 + dz), x + (2 + dx)] += part

    @pl.when((z == pl.num_programs(0) - 1) & (xb == pl.num_programs(1) - 1))
    def _():
        spot = lax.broadcasted_iota(jnp.int32, (across, lanes), 1)
        blocks = out_ref.shape[0]
        deep = out_ref.shape[3]

        def finish(p, _):
            for k in range(8):
                up = pltpu.roll(plus[p, pl.ds(2, across), k, :], 1, 1)
                down = pltpu.roll(minus[p, pl.ds(2, across), k, :], lanes - 1, 1)
                whole = mid[p, pl.ds(2, across), k, :]
                whole = whole + jnp.where(spot >= 1, up, 0.0)
                whole = whole + jnp.where(spot < lanes - 1, down, 0.0)
                upright = whole.T
                for b in range(blocks):
                    out_ref[b, k, p] = upright[b * deep : (b + 1) * deep]
            return 0

        lax.fori_loop(0, planes, finish, 0)


def local_moments(state, table, blocks):
    modes, nz, nx, ny = state.shape
    width = math.gcd(nx, 16)
    acc = pltpu.VMEM((nz + 4, nx + 4, 8, ny), jnp.float32)
    shape = (blocks, 8, nz + 4, ny // blocks, nx)
    return pl.pallas_call(
        moments_kernel,
        grid=(nz, nx // width),
        in_specs=[
            pl.BlockSpec((modes, 1, width, ny), lambda z, x: (0, z, x, 0)),
            pl.BlockSpec(table.shape, lambda z, x: (0, 0)),
        ],
        out_specs=pl.BlockSpec(shape, lambda z, x: (0, 0, 0, 0, 0)),
        out_shape=jax.ShapeDtypeStruct(shape, jnp.float32),
        scratch_shapes=[acc, acc, acc],
        compiler_params=pltpu.CompilerParams(
            dimension_semantics=("arbitrary", "arbitrary"), vmem_limit_bytes=60 * 1024 * 1024
        ),
        name="moments",
    )(state, table)


def heat_kernel(s_ref, m_ref, t_ref, k_ref, temp_ref, flux_ref):
    ny, nx = t_ref.shape[1:]

    def shift(v, axis, step):
        if axis == 0:
            zero = jnp.zeros((1,) + v.shape[1:], v.dtype)
            return jnp.concatenate([v[1:], zero] if step > 0 else [zero, v[:-1]], axis=0)
        size = v.shape[axis]
        return pltpu.roll(v, (size - 1) if step > 0 else 1, axis)

    kappa = k_ref[...]
    inside = kappa > 0.0
    start = t_ref[...]
    total = s_ref[0]

    def harmonic(first, second):
        summed = first + second
        positive = summed > 0.0
        return jnp.where(positive, 2.0 * first * second / jnp.where(positive, summed, 1.0), 0.0)

    ahead = [harmonic(kappa, shift(kappa, axis, 1)) for axis in (2, 1, 0)]

    def operator(v):
        spread = None
        for axis, face in zip((2, 1, 0), ahead):
            flow = face * (shift(v, axis, 1) - v)
            term = flow - shift(flow, axis, -1)
            spread = term if spread is None else spread + term
        return total * v - spread

    def solve(flux):
        rhs = None
        for axis, f in zip((2, 1, 0), flux):
            term = shift(f, axis, 1) - shift(f, axis, -1)
            rhs = term if rhs is None else rhs + term
        rhs = rhs * -0.5
        theta = total + 6.0 * kappa_top
        spread = 6.0 * kappa_top
        sigma = theta / spread
        rho = 1.0 / sigma
        residual = rhs
        direction = rhs / theta
        correction = direction
        for _ in range(SWEEPS - 1):
            residual = residual - operator(direction)
            rho_next = 1.0 / (2.0 * sigma - rho)
            direction = rho_next * rho * direction + 2.0 * rho_next / spread * residual
            rho = rho_next
            correction = correction + direction
        return correction

    first = [m_ref[k] + s_ref[1 + k] * start for k in range(4)]
    middle = jnp.where(inside, first[0] / total + solve(first[1:]), 0.0)
    moved = [start] + [shift(start, 2 - axis, -step) for axis in range(3) for step in (1, -1)]
    second = []
    for k in range(4):
        value = m_ref[4 + k] + s_ref[1 + k] * middle
        for n, m in enumerate(moved):
            value = value + s_ref[5 + 7 * k + n] * m
        second.append(jnp.where(inside, value, 0.0))
    temp_ref[...] = second[0] / total + solve(second[1:])
    for a in range(3):
        flux_ref[a] = second[1 + a]


def heat(scalars, moments, temp, kappa):
    shape = temp.shape
    return pl.pallas_call(
        heat_kernel,
        in_specs=[pl.BlockSpec(memory_space=pltpu.SMEM)]
        + [pl.BlockSpec(memory_space=pltpu.VMEM)] * 3,
        out_specs=[pl.BlockSpec(memory_space=pltpu.VMEM)] * 2,
        out_shape=[
            jax.ShapeDtypeStruct(shape, jnp.float32),
            jax.ShapeDtypeStruct((3,) + shape, jnp.float32),
        ],
        compiler_params=pltpu.CompilerParams(vmem_limit_bytes=60 * 1024 * 1024),
        name="heat",
    )(scalars, moments, temp, kappa)


def widen(cells, sides, width):
    for axis, dim in sides:
        count = lax.axis_size(axis)
        ends = count - 1
        head = lax.slice_in_dim(cells, 0, width, axis=dim)
        tail = lax.slice_in_dim(cells, cells.shape[dim] - width, cells.shape[dim], axis=dim)
        cells = jnp.concatenate(
            [
                lax.ppermute(tail, axis, [(i, i + 1) for i in range(ends)]),
                cells,
                lax.ppermute(head, axis, [(i + 1, i) for i in range(ends)]),
            ],
            axis=dim,
        )
    return cells


def per_device(
    excess_phonon_enthalpy,
    thermal_offset,
    state_specific_warmth_scaled,
    scattering_lifetimes,
    state_polarization_label,
    state_orientation_label,
    polarization_propagation_rate,
    thermal_conductance_bulk,
    substance_label,
):
    groups = lax.axis_size("mode")
    slabs = lax.axis_size("space")
    modes = state_orientation_label.shape[0]
    velocity, rates, capacity = mode_table(
        state_polarization_label,
        state_orientation_label,
        state_specific_warmth_scaled,
        scattering_lifetimes,
        polarization_propagation_rate,
        modes * groups,
    )
    once, twice = stencils(velocity, rates)
    weights = jnp.stack([rates, *velocity])
    gain = time_step * rates * capacity
    sums = jnp.concatenate(
        [
            jnp.sum(capacity * rates)[None],
            jnp.sum(weights * gain, axis=1),
            jnp.sum((weights * gain)[:, None, :] * once[None], axis=2).reshape(-1),
        ]
    )
    scalars = lax.psum(sums, "mode")

    lone = jnp.zeros((len(TWO), modes), jnp.float32)
    table = jnp.stack([jnp.concatenate([once, lone]), twice], axis=1)
    table = (table[:, :, None, :] * weights[None, None]).reshape(8 * len(OFFSETS), modes)
    high = table.astype(jnp.bfloat16)
    low = (table - high.astype(jnp.float32)).astype(jnp.bfloat16)
    table = jnp.concatenate([high, low], axis=1)

    kappa = thermal_conductance_bulk * jnp.where(substance_label == 1, pore_factor, 1.0)
    sides = (("space", 3), ("mode", 2))
    start = jnp.transpose(jnp.stack([thermal_offset, kappa]), (0, 3, 2, 1))
    start = widen(start, sides, HALO)

    partial = local_moments(excess_phonon_enthalpy, table, groups)
    reduced = lax.psum_scatter(partial, "mode", scatter_dimension=0, tiled=True)[0]
    _, deep, ny, nx = reduced.shape
    nz = deep - 4
    part = nx // slabs
    cut = reduced.reshape(8, deep, ny, slabs, part)
    cut = jnp.transpose(cut, (3, 0, 1, 2, 4))
    cut = lax.all_to_all(cut, "space", split_axis=0, concat_axis=0, tiled=True)
    height = nz * slabs
    summed = None
    for s in range(slabs):
        term = jnp.pad(cut[s], ((0, 0), (s * nz, height - (s + 1) * nz), (0, 0), (0, 0)))
        summed = term if summed is None else summed + term
    summed = summed[:, 2:-2]
    moments = widen(summed, sides, HALO)

    def fill(values):
        extra = -values.shape[-1] % 128
        return jnp.pad(values, ((0, 0),) * (values.ndim - 1) + ((0, extra),))

    temp, flux = heat(scalars, fill(moments), fill(start[0]), fill(start[1]))
    rows = slice(HALO, HALO + ny)
    columns = slice(HALO, HALO + part)
    return (
        jnp.transpose(temp[:, rows, columns], (2, 1, 0)),
        jnp.transpose(flux[:, :, rows, columns], (0, 3, 2, 1)),
    )


def solution(mesh):
    placed = (
        P("mode", "space", None, None),
        P("space", "mode", None),
        P("mode"),
        P("mode"),
        P("mode"),
        P("mode"),
        P(),
        P("space", "mode", None),
        P("space", "mode", None),
    )
    return jax.shard_map(
        per_device,
        mesh=mesh,
        in_specs=placed,
        out_specs=(P("space", "mode", None), P(None, "space", "mode", None)),
        check_vma=False,
    )
```

time: 1080 us -> 288 us (0.27)
  the two profiles are of different devices: /device:TPU:1 before, /device:TPU:14 now
where the time goes in v1:
time: 288 us; the launch traced here: 286 us
  waiting for transfers between devices  103 us (36%)
  Pallas kernels  74.1 us (26%)
  local copies, waits for them, and re-layouts  42.9 us (15%)
  starting transfers between devices  22.3 us (8%)
  other arithmetic  16 us (6%)
  between operations  14.4 us (5%)
  blocking collectives  13.4 us (5%)
    reduce_scatter x1, waiting for transfers between devices, per_device(): lax.psum_scatter(partial, 'mode', scatter_dimension=0, tiled=True)[0]  66.6 us
    pallas_call x1, Pallas kernels, local_moments(): pl.pallas_call(moments_kernel, grid=(nz, nx // width), in_specs=[pl.Block...  65.6 us
    ppermute x4, waiting for transfers between devices, widen(): lax.ppermute(tail, axis, [(i, i + 1) for i in range(ends)])  26 us
    psum x1, blocking collectives, per_device(): scalars = lax.psum(sums, 'mode')  13.4 us
    unnamed x25, local copies, waits for them, and re-layouts  11.3 us
    ppermute x4, starting transfers between devices, widen(): lax.ppermute(head, axis, [(i + 1, i) for i in range(ends)])  10.7 us
    ppermute x4, waiting for transfers between devices, widen(): lax.ppermute(head, axis, [(i + 1, i) for i in range(ends)])  10.1 us
    pallas_call x1, Pallas kernels, heat(): pl.pallas_call(heat_kernel, in_specs=[pl.BlockSpec(memory_space=pltpu.SME...  8.52 us
  transfers between devices with their start and end apart: 10, of which 6 were waited for; matrix products, arithmetic and copies ran while one was open for 6% of the time, Pallas kernels for 0%

profile of v1, /device:TPU:14, one launch (start us, length us, event | category | flops | bytes accessed | tf_op | source)
XLA Modules:
  0.0 285.8 jit_solution(15823949201590588587)
XLA Ops:
  7.2 0.8 select_reduce_fusion
  8.0 0.7 multiply_bitcast_fusion.1
  8.6 0.7 multiply_bitcast_fusion.3
  9.4 0.7 multiply_bitcast_fusion.4
  10.4 1.3 multiply_reduce_fusion.1
  11.8 0.7 pad_maximum_fusion.3.a_ref
  12.6 65.6 %moments.1 = f32[8,8,12,16,128]{4,3,2,1,0:T(8,128)} custom-call(bf16[96,8,128,128]{3,2,1,0:T(8,128)(2,1)} %e_ref.1, bf16[200,192]{1,0:T(8,128)(2,1)} %pad_maximum_fusion.3.a_ref), custom_call_target="tpu_custom_call" | custom-call | tf_op jit(solution)/shard_map/moments/pallas_call | solution.py:117
  78.2 0.9 copy-done.6
  79.9 66.6 %reduce-scatter.2.cloned.1.call-done = f32[1,8,12,16,128]{4,3,2,1,0:T(8,128)} async-done(((f32[8,8,12,16,128]{4,3,2,1,0:T(8,128)}), f32[1,8,12,16,128]{4,3,2,1,0:T(8,128)}) %reduce-scatter.2.cloned.1.call-update) | async-done | bytes 786448 | tf_op jit(solution)/shard_map/reduce_scatter | solution.py:279
  146.4 3.6 %reshape_squeeze.3 = f32[8,12,16,4,32]{4,3,2,1,0:T(4,128)} reshape(f32[1,8,12,16,128]{4,3,2,1,0:T(8,128)} %reduce-scatter.2.cloned.1.call-done) | data formatting | bytes 1572864 | tf_op jit(solution)/shard_map/reshape;squeeze | solution.py:283
  150.1 4.0 %copy.48 = f32[8,12,16,4,32]{4,2,1,0,3:T(8,128)} copy(f32[8,12,16,4,32]{4,3,2,1,0:T(4,128)} %reshape_squeeze.3) | data formatting | bytes 1572864 | tf_op jit(solution)/shard_map/reshape;squeeze | solution.py:283
  154.0 4.4 %reshape.60 = f32[4,1,49152]{2,1,0:T(1,128)} reshape(f32[4,8,12,16,32]{4,3,2,1,0:T(8,128)} %bitcast.96) | data formatting | bytes 1572864
  158.4 4.2 %all-to-all-start = ((f32[4,1,49152]{2,1,0:T(1,128)}), f32[4,1,49152]{2,1,0:T(1,128)S(1)}, u32[]{:S(2)}, u32[]{:S(2)}) async-start(f32[4,1,49152]{2,1,0:T(1,128)} %reshape.60), calls=%async_computation.1 | async-start | bytes 1572864 | tf_op jit(solution)/shard_map/all_to_all | solution.py:285
  162.8 2.5 collective-permute-start.5
  165.3 1.3 collective-permute-start.4
  166.9 0.7 pad_maximum_fusion.6
  167.6 13.4 %psum.7.s_ref = f32[33]{0:T(128)} all-reduce(f32[33]{0:T(128)S(1)} %pad_maximum_fusion.6), channel_id=1, replica_groups=mesh['space'=4,'mode'=8] {'mode'}, use_global_device_ids=true, to_apply=%region_4.5 | all-reduce | flops 33 | bytes 264 | tf_op jit(solution)/shard_map/psum | solution.py:264
  180.9 2.4 collective-permute-done.5
  183.4 12.2 %collective-permute-done.4 = f32[2,32,16,8]{3,2,1,0:T(8,128)S(1)} collective-permute-done((f32[2,32,16,8]{3,2,1,0:T(8,128)S(1)}, f32[2,32,16,8]{3,2,1,0:T(8,128)S(1)}, u32[]{:S(2)}, u32[]{:S(2)}) %collective-permute-start.4) | collective-permute-done | bytes 32800 | tf_op jit(solution)/shard_map/ppermute | solution.py:223
  196.4 0.5 broadcast.263
  196.9 2.9 %reduce = f32[4,49152]{1,0:T(4,128)S(1)} reduce(f32[4,1,49152]{2,1,0:T(1,128)S(1)} %all-to-all-done, f32[]{:T(128)} %broadcast.263), dimensions={1}, to_apply=%all_to_all.3.reduce_sub_computation | reduce | bytes 1572868 | tf_op jit(solution)/shard_map/all_to_all | solution.py:285
  199.8 2.7 reshape.61
  202.5 2.1 slice_bitcast_fusion.3
  204.9 2.7 fusion.14
  207.6 3.1 %copy.39 = f32[8,32,16,8]{1,3,2,0:T(8,128)} copy(f32[8,32,16,8]{3,2,1,0:T(8,128)} %get-tuple-element.36) | data formatting | bytes 262144 | tf_op jit(solution)/shard_map/slice | solution.py:219
  210.7 4.2 %collective-permute-start.1 = (f32[8,32,16,8]{1,3,2,0:T(8,128)}, f32[8,32,16,8]{1,3,2,0:T(8,128)}, u32[]{:S(2)}, u32[]{:S(2)}) collective-permute-start(f32[8,32,16,8]{1,3,2,0:T(8,128)} %copy.39), channel_id=1, source_target_pairs={{8,0},{16,8},{24,16},{9,1},{17,9},{25,17},{10,2},{18,10},{26,18},{... | collective-permute-start | bytes 393224 | tf_op jit(solution)/shard_map/ppermute | solution.py:225
  214.9 3.1 %copy.38 = f32[8,32,16,8]{1,3,2,0:T(8,128)} copy(f32[8,32,16,8]{3,2,1,0:T(8,128)} %get-tuple-element.35) | data formatting | bytes 262144 | tf_op jit(solution)/shard_map/slice | solution.py:220
  218.0 1.3 collective-permute-start
  219.3 0.8 fusion.16
  220.2 1.9 collective-permute-start.7
  222.1 2.4 collective-permute-start.6
  224.5 1.5 slice.75
  226.0 1.9 copy.41
  227.9 9.9 %collective-permute-done = f32[8,32,16,8]{1,3,2,0:T(8,128)} collective-permute-done((f32[8,32,16,8]{1,3,2,0:T(8,128)}, f32[8,32,16,8]{1,3,2,0:T(8,128)}, u32[]{:S(2)}, u32[]{:S(2)}) %collective-permute-start) | collective-permute-done | bytes 131104 | tf_op jit(solution)/shard_map/ppermute | solution.py:223
  237.8 3.1 %copy.40 = f32[8,32,16,8]{3,2,1,0:T(8,128)} copy(f32[8,32,16,8]{1,3,2,0:T(8,128)} %collective-permute-done) | data formatting | bytes 262144 | tf_op jit(solution)/shard_map/ppermute | solution.py:223
  240.9 3.4 %pad_maximum_fusion = f32[8,32,16,48]{3,2,1,0:T(8,128)S(1)} fusion(f32[8,32,16,8]{3,2,1,0:T(8,128)S(1)} %copy.41, f32[8,32,16,32]{3,2,1,0:T(8,128)} %slice.75, f32[8,32,16,8]{3,2,1,0:T(8,128)} %copy.40), kind=kLoop, calls=%fused_computation.10 | loop fusion | flops 393216 | bytes 1572864 | tf_op jit(solution)/shard_map/concatenate | solution.py:221
  244.5 2.1 collective-permute-start.3
  246.6 2.4 collective-permute-start.2
  249.5 0.8 pad.32.t_ref
  250.3 0.9 pad.33.k_ref
  251.2 7.7 %collective-permute-done.3 = f32[8,32,8,48]{3,2,1,0:T(8,128)S(1)} collective-permute-done((f32[8,32,8,48]{3,2,1,0:T(8,128)S(1)}, f32[8,32,8,48]{3,2,1,0:T(8,128)S(1)}, u32[]{:S(2)}, u32[]{:S(2)}) %collective-permute-start.3) | collective-permute-done | bytes 393248 | tf_op jit(solution)/shard_map/ppermute | solution.py:225
  258.9 3.8 %collective-permute-done.2 = f32[8,32,8,48]{3,2,1,0:T(8,128)S(1)} collective-permute-done((f32[8,32,8,48]{3,2,1,0:T(8,128)S(1)}, f32[8,32,8,48]{3,2,1,0:T(8,128)S(1)}, u32[]{:S(2)}, u32[]{:S(2)}) %collective-permute-start.2) | collective-permute-done | bytes 393248 | tf_op jit(solution)/shard_map/ppermute | solution.py:223
  262.7 2.9 %select_maximum_fusion.m_ref = f32[8,32,32,128]{3,2,1,0:T(8,128)} fusion(f32[8,32,8,48]{3,2,1,0:T(8,128)S(1)} %collective-permute-done.3, f32[8,32,8,48]{3,2,1,0:T(8,128)S(1)} %collective-permute-done.2, f32[8,32,16,8]{3,2,1,0:T(8,128)S(1)} %copy.41, f32[8,32,16,32]{3,2,1,0:T(8,128)S(1)} %copy-done.1, f32[8,32,16,8]{3,2,1,0:T(8,128)S(1)} %copy-done), kind=kLoop, calls=%fused_computation | loop fusion | flops 10485760 | bytes 5767168 | tf_op jit(solution)/shard_map/concatenate | solution.py:221
  265.7 8.5 %heat.1 = (f32[32,32,128]{2,1,0:T(8,128)}, f32[3,32,32,128]{3,2,1,0:T(8,128)}) custom-call(f32[33]{0:T(128)} %psum.7.s_ref, f32[8,32,32,128]{3,2,1,0:T(8,128)} %select_maximum_fusion.m_ref, f32[32,32,128]{2,1,0:T(8,128)} %pad.32.t_ref, f32[32,32,128]{2,1,0:T(8,128)} %pad.33.k_ref), custom_call_target="tpu_custom_call" | custom-call | tf_op jit(solution)/shard_map/heat/pallas_call | solution.py:201
  274.2 1.1 slice_bitcast_fusion.7
  275.3 0.9 copy.45
  276.1 1.4 slice_bitcast_fusion.4
  277.6 1.4 copy.46
  (48 shorter events, 3.4 us)
Async XLA Ops:
  7.2 139.3 %reduce-scatter.2.cloned.1.call-start = ((), (), s32[]{:S(2)}) async-start(), calls=%async_computation.2 | async-start | bytes 7077888 | tf_op jit(solution)/shard_map/reduce_scatter | solution.py:279
  78.2 0.9 copy-start.6
  78.2 1.1 copy-start.7
  78.2 1.4 copy-start.8
  158.4 37.5 %all-to-all-start = ((f32[4,1,49152]{2,1,0:T(1,128)}), f32[4,1,49152]{2,1,0:T(1,128)S(1)}, u32[]{:S(2)}, u32[]{:S(2)}) async-start(f32[4,1,49152]{2,1,0:T(1,128)} %reshape.60), calls=%async_computation.1 | async-start | bytes 1572864 | tf_op jit(solution)/shard_map/all_to_all | solution.py:285
  162.8 20.6 %collective-permute-start.5 = (f32[2,32,16,8]{3,2,1,0:T(8,128)S(1)}, f32[2,32,16,8]{3,2,1,0:T(8,128)S(1)}, u32[]{:S(2)}, u32[]{:S(2)}) collective-permute-start(f32[2,32,16,8]{3,2,1,0:T(8,128)S(1)} %get-tuple-element.44), channel_id=1, source_target_pairs={{8,0},{16,8},{24,16},{9,1},{17,9},{25,17},{10,2},{18,10},{26,18},{... | collective-permute-start | bytes 98312 | tf_op jit(solution)/shard_map/ppermute | solution.py:225
  165.3 30.3 %collective-permute-start.4 = (f32[2,32,16,8]{3,2,1,0:T(8,128)S(1)}, f32[2,32,16,8]{3,2,1,0:T(8,128)S(1)}, u32[]{:S(2)}, u32[]{:S(2)}) collective-permute-start(f32[2,32,16,8]{3,2,1,0:T(8,128)S(1)} %get-tuple-element.43), channel_id=1, source_target_pairs={{0,8},{8,16},{16,24},{1,9},{9,17},{17,25},{2,10},{10,18},{18,26},{... | collective-permute-start | bytes 98312 | tf_op jit(solution)/shard_map/ppermute | solution.py:223
  183.4 12.6 %copy-start.2 = (f32[2,32,16,8]{3,2,1,0:T(8,128)}, f32[2,32,16,8]{3,2,1,0:T(8,128)S(1)}, u32[]{:S(2)}) copy-start(f32[2,32,16,8]{3,2,1,0:T(8,128)S(1)} %collective-permute-done.5) | copy-start | bytes 98308
  195.6 0.8 copy-start.4
  210.7 15.3 %collective-permute-start.1 = (f32[8,32,16,8]{1,3,2,0:T(8,128)}, f32[8,32,16,8]{1,3,2,0:T(8,128)}, u32[]{:S(2)}, u32[]{:S(2)}) collective-permute-start(f32[8,32,16,8]{1,3,2,0:T(8,128)} %copy.39), channel_id=1, source_target_pairs={{8,0},{16,8},{24,16},{9,1},{17,9},{25,17},{10,2},{18,10},{26,18},{... | collective-permute-start | bytes 393224 | tf_op jit(solution)/shard_map/ppermute | solution.py:225
  218.0 19.8 %collective-permute-start = (f32[8,32,16,8]{1,3,2,0:T(8,128)}, f32[8,32,16,8]{1,3,2,0:T(8,128)}, u32[]{:S(2)}, u32[]{:S(2)}) collective-permute-start(f32[8,32,16,8]{1,3,2,0:T(8,128)} %copy.38), channel_id=1, source_target_pairs={{0,8},{8,16},{16,24},{1,9},{9,17},{17,25},{2,10},{10,18},{18,26},{... | collective-permute-start | bytes 393224 | tf_op jit(solution)/shard_map/ppermute | solution.py:223
  220.2 28.8 %collective-permute-start.7 = (f32[2,32,8,48]{3,2,1,0:T(8,128)}, f32[2,32,8,48]{3,2,1,0:T(8,128)S(1)}, u32[]{:S(2)}, u32[]{:S(2)}) collective-permute-start(f32[2,32,8,48]{3,2,1,0:T(8,128)} %get-tuple-element.42), channel_id=1, source_target_pairs={{1,0},{2,1},{3,2},{4,3},{5,4},{6,5},{7,6},{9,8},{10,9},{11,10},{12... | collective-permute-start | bytes 294920 | tf_op jit(solution)/shard_map/ppermute | solution.py:225
  222.1 26.9 %collective-permute-start.6 = (f32[2,32,8,48]{3,2,1,0:T(8,128)}, f32[2,32,8,48]{3,2,1,0:T(8,128)S(1)}, u32[]{:S(2)}, u32[]{:S(2)}) collective-permute-start(f32[2,32,8,48]{3,2,1,0:T(8,128)} %get-tuple-element.41), channel_id=1, source_target_pairs={{0,1},{1,2},{2,3},{3,4},{4,5},{5,6},{6,7},{8,9},{9,10},{10,11},{11... | collective-permute-start | bytes 294920 | tf_op jit(solution)/shard_map/ppermute | solution.py:223
  244.3 4.7 %copy-start.3 = (f32[2,32,16,8]{3,2,1,0:T(8,128)S(1)}, f32[2,32,16,8]{3,2,1,0:T(8,128)}, u32[]{:S(2)}) copy-start(f32[2,32,16,8]{3,2,1,0:T(8,128)} %copy-done.2) | copy-start | bytes 98308
  244.3 4.7 %copy-start.5 = (f32[2,32,16,8]{3,2,1,0:T(8,128)S(1)}, f32[2,32,16,8]{3,2,1,0:T(8,128)}, u32[]{:S(2)}) copy-start(f32[2,32,16,8]{3,2,1,0:T(8,128)} %copy-done.4) | copy-start | bytes 98308
  244.5 14.4 %collective-permute-start.3 = (f32[8,32,8,48]{3,2,1,0:T(8,128)S(1)}, f32[8,32,8,48]{3,2,1,0:T(8,128)S(1)}, u32[]{:S(2)}, u32[]{:S(2)}) collective-permute-start(f32[8,32,8,48]{3,2,1,0:T(8,128)S(1)} %get-tuple-element.38), channel_id=1, source_target_pairs={{1,0},{2,1},{3,2},{4,3},{5,4},{6,5},{7,6},{9,8},{10,9},{11,10},{12... | collective-permute-start | bytes 1179656 | tf_op jit(solution)/shard_map/ppermute | solution.py:225
  246.6 16.1 %collective-permute-start.2 = (f32[8,32,8,48]{3,2,1,0:T(8,128)S(1)}, f32[8,32,8,48]{3,2,1,0:T(8,128)S(1)}, u32[]{:S(2)}, u32[]{:S(2)}) collective-permute-start(f32[8,32,8,48]{3,2,1,0:T(8,128)S(1)} %get-tuple-element.37), channel_id=1, source_target_pairs={{0,1},{1,2},{2,3},{3,4},{4,5},{5,6},{6,7},{8,9},{9,10},{10,11},{11... | collective-permute-start | bytes 1179656 | tf_op jit(solution)/shard_map/ppermute | solution.py:223
  249.4 13.3 %copy-start = (f32[8,32,16,8]{3,2,1,0:T(8,128)S(1)}, f32[8,32,16,8]{3,2,1,0:T(8,128)}, u32[]{:S(2)}) copy-start(f32[8,32,16,8]{3,2,1,0:T(8,128)} %copy.40) | copy-start | bytes 393220
  249.4 13.3 %copy-start.1 = (f32[8,32,16,32]{3,2,1,0:T(8,128)S(1)}, f32[8,32,16,32]{3,2,1,0:T(8,128)}, u32[]{:S(2)}) copy-start(f32[8,32,16,32]{3,2,1,0:T(8,128)} %slice.75) | copy-start | bytes 1572868
Sparse Core Ops, SparseCore 0:
  78.4 68.0 reduce-scatter.1

commit v2 on v1

--- a/solution.py
+++ b/solution.py
@@ -52,7 +52,7 @@
     return jnp.stack(once), jnp.stack(twice)
 
 
-def moments_kernel(e_ref, a_ref, out_ref, mid, plus, minus):
+def moments_kernel(place_ref, e_ref, a_ref, sums_ref, out_ref, mid, plus, minus):
     z = pl.program_id(0)
     xb = pl.program_id(1)
     width = e_ref.shape[2]
@@ -94,32 +94,57 @@
         blocks = out_ref.shape[0]
         deep = out_ref.shape[3]
 
-        def finish(p, _):
+        row = lax.broadcasted_iota(jnp.int32, (lanes, across), 0)
+        column = lax.broadcasted_iota(jnp.int32, (lanes, across), 1)
+
+        def put(k, p, value):
+            for b in range(blocks):
+                out_ref[b, k, p] = value[b * deep : (b + 1) * deep]
+
+        def difference(value, axis):
+            spots = (row, column)[axis]
+            size = value.shape[axis]
+            after = jnp.where(spots < size - 1, pltpu.roll(value, size - 1, axis), 0.0)
+            return after - jnp.where(spots >= 1, pltpu.roll(value, 1, axis), 0.0)
+
+        def finish(p, below):
+            upright = []
             for k in range(8):
                 up = pltpu.roll(plus[p, pl.ds(2, across), k, :], 1, 1)
                 down = pltpu.roll(minus[p, pl.ds(2, across), k, :], lanes - 1, 1)
                 whole = mid[p, pl.ds(2, across), k, :]
                 whole = whole + jnp.where(spot >= 1, up, 0.0)
                 whole = whole + jnp.where(spot < lanes - 1, down, 0.0)
-                upright = whole.T
-                for b in range(blocks):
-                    out_ref[b, k, p] = upright[b * deep : (b + 1) * deep]
-            return 0
-
-        lax.fori_loop(0, planes, finish, 0)
-
-
-def local_moments(state, table, blocks):
+                upright.append(whole.T)
+            put(0, p, upright[0])
+            inside = (p >= place_ref[0]) & (p < place_ref[1])
+            flux = [jnp.where(inside, v, 0.0) for v in upright[1:4]]
+            put(1, p, difference(flux[0], 1) + difference(flux[1], 0) - below)
+            under = jnp.maximum(p - 1, 0)
+            for b in range(blocks):
+                out_ref[b, 1, under] += flux[2][b * deep : (b + 1) * deep]
+            for k in range(4):
+                put(2 + k, p, upright[4 + k])
+            return flux[2]
+
+        lax.fori_loop(0, planes, finish, jnp.zeros((lanes, across), jnp.float32))
+        for b in range(blocks):
+            out_ref[b, 0, 0] = jnp.broadcast_to(sums_ref[...], (deep, across))
+
+
+def local_moments(place, state, table, sums, blocks):
     modes, nz, nx, ny = state.shape
     width = math.gcd(nx, 16)
     acc = pltpu.VMEM((nz + 4, nx + 4, 8, ny), jnp.float32)
-    shape = (blocks, 8, nz + 4, ny // blocks, nx)
+    shape = (blocks, 6, nz + 4, ny // blocks, nx)
     return pl.pallas_call(
         moments_kernel,
         grid=(nz, nx // width),
         in_specs=[
+            pl.BlockSpec(memory_space=pltpu.SMEM),
             pl.BlockSpec((modes, 1, width, ny), lambda z, x: (0, z, x, 0)),
             pl.BlockSpec(table.shape, lambda z, x: (0, 0)),
+            pl.BlockSpec(sums.shape, lambda z, x: (0, 0)),
         ],
         out_specs=pl.BlockSpec(shape, lambda z, x: (0, 0, 0, 0, 0)),
         out_shape=jax.ShapeDtypeStruct(shape, jnp.float32),
@@ -128,18 +153,24 @@
             dimension_semantics=("arbitrary", "arbitrary"), vmem_limit_bytes=60 * 1024 * 1024
         ),
         name="moments",
-    )(state, table)
-
-
-def heat_kernel(s_ref, m_ref, t_ref, k_ref, temp_ref, flux_ref):
-    ny, nx = t_ref.shape[1:]
+    )(place, state, table, sums)
+
+
+def heat_kernel(s_ref, m_ref, low_ref, high_ref, t_ref, k_ref, temp_ref, flux_ref):
+    lane = lax.broadcasted_iota(jnp.int32, t_ref.shape, 2)
 
     def shift(v, axis, step):
         if axis == 0:
             zero = jnp.zeros((1,) + v.shape[1:], v.dtype)
             return jnp.concatenate([v[1:], zero] if step > 0 else [zero, v[:-1]], axis=0)
         size = v.shape[axis]
-        return pltpu.roll(v, (size - 1) if step > 0 else 1, axis)
+        moved = pltpu.roll(v, (size - 1) if step > 0 else 1, axis)
+        if axis == 2:
+            moved = jnp.where(lane < size - 1 if step > 0 else lane >= 1, moved, 0.0)
+        return moved
+
+    def field(k):
+        return jnp.concatenate([low_ref[k], m_ref[k], high_ref[k]], axis=1)
 
     kappa = k_ref[...]
     inside = kappa > 0.0
@@ -161,11 +192,9 @@
             spread = term if spread is None else spread + term
         return total * v - spread
 
-    def solve(flux):
-        rhs = None
+    def solve(flux, rhs=0.0):
         for axis, f in zip((2, 1, 0), flux):
-            term = shift(f, axis, 1) - shift(f, axis, -1)
-            rhs = term if rhs is None else rhs + term
+            rhs = rhs + (shift(f, axis, 1) - shift(f, axis, -1))
         rhs = rhs * -0.5
         theta = total + 6.0 * kappa_top
         spread = 6.0 * kappa_top
@@ -182,26 +211,28 @@
             correction = correction + direction
         return correction
 
-    first = [m_ref[k] + s_ref[1 + k] * start for k in range(4)]
-    middle = jnp.where(inside, first[0] / total + solve(first[1:]), 0.0)
+    weight = field(0) + s_ref[1] * start
+    change = solve([s_ref[2 + a] * start for a in range(3)], field(1))
+    middle = jnp.where(inside, weight / total + change, 0.0)
     moved = [start] + [shift(start, 2 - axis, -step) for axis in range(3) for step in (1, -1)]
     second = []
     for k in range(4):
-        value = m_ref[4 + k] + s_ref[1 + k] * middle
+        value = field(2 + k) + s_ref[1 + k] * middle
         for n, m in enumerate(moved):
             value = value + s_ref[5 + 7 * k + n] * m
         second.append(jnp.where(inside, value, 0.0))
-    temp_ref[...] = second[0] / total + solve(second[1:])
+    rows = slice(HALO, t_ref.shape[1] - HALO)
+    temp_ref[...] = (second[0] / total + solve(second[1:]))[:, rows]
     for a in range(3):
-        flux_ref[a] = second[1 + a]
-
-
-def heat(scalars, moments, temp, kappa):
-    shape = temp.shape
+        flux_ref[a] = second[1 + a][:, rows]
+
+
+def heat(scalars, moments, low, high, temp, kappa):
+    shape = moments.shape[1:]
     return pl.pallas_call(
         heat_kernel,
         in_specs=[pl.BlockSpec(memory_space=pltpu.SMEM)]
-        + [pl.BlockSpec(memory_space=pltpu.VMEM)] * 3,
+        + [pl.BlockSpec(memory_space=pltpu.VMEM)] * 5,
         out_specs=[pl.BlockSpec(memory_space=pltpu.VMEM)] * 2,
         out_shape=[
             jax.ShapeDtypeStruct(shape, jnp.float32),
@@ -209,24 +240,17 @@
         ],
         compiler_params=pltpu.CompilerParams(vmem_limit_bytes=60 * 1024 * 1024),
         name="heat",
-    )(scalars, moments, temp, kappa)
-
-
-def widen(cells, sides, width):
-    for axis, dim in sides:
-        count = lax.axis_size(axis)
-        ends = count - 1
-        head = lax.slice_in_dim(cells, 0, width, axis=dim)
-        tail = lax.slice_in_dim(cells, cells.shape[dim] - width, cells.shape[dim], axis=dim)
-        cells = jnp.concatenate(
-            [
-                lax.ppermute(tail, axis, [(i, i + 1) for i in range(ends)]),
-                cells,
-                lax.ppermute(head, axis, [(i + 1, i) for i in range(ends)]),
-            ],
-            axis=dim,
-        )
-    return cells
+    )(scalars, moments, low, high, temp, kappa)
+
+
+def beside(cells, dim, width):
+    ends = lax.axis_size("mode") - 1
+    head = lax.slice_in_dim(cells, 0, width, axis=dim)
+    tail = lax.slice_in_dim(cells, cells.shape[dim] - width, cells.shape[dim], axis=dim)
+    return (
+        lax.ppermute(tail, "mode", [(i, i + 1) for i in range(ends)]),
+        lax.ppermute(head, "mode", [(i + 1, i) for i in range(ends)]),
+    )
 
 
 def per_device(
@@ -261,47 +285,42 @@
             jnp.sum((weights * gain)[:, None, :] * once[None], axis=2).reshape(-1),
         ]
     )
-    scalars = lax.psum(sums, "mode")
 
     lone = jnp.zeros((len(TWO), modes), jnp.float32)
     table = jnp.stack([jnp.concatenate([once, lone]), twice], axis=1)
     table = (table[:, :, None, :] * weights[None, None]).reshape(8 * len(OFFSETS), modes)
-    high = table.astype(jnp.bfloat16)
-    low = (table - high.astype(jnp.float32)).astype(jnp.bfloat16)
-    table = jnp.concatenate([high, low], axis=1)
+    high = lax.reduce_precision(table, 8, 7)
+    table = jnp.concatenate([high, table - high], axis=1).astype(jnp.bfloat16)
 
     kappa = thermal_conductance_bulk * jnp.where(substance_label == 1, pore_factor, 1.0)
-    sides = (("space", 3), ("mode", 2))
-    start = jnp.transpose(jnp.stack([thermal_offset, kappa]), (0, 3, 2, 1))
-    start = widen(start, sides, HALO)
-
-    partial = local_moments(excess_phonon_enthalpy, table, groups)
+    start = jnp.transpose(jnp.stack([thermal_offset, kappa]), (0, 3, 1, 2))
+    start = jnp.transpose(lax.all_gather(start, "space", axis=2, tiled=True), (0, 1, 3, 2))
+    low, high = beside(start, 2, HALO)
+    start = jnp.concatenate([low, start, high], axis=2)
+
+    nz, nx, ny = excess_phonon_enthalpy.shape[1:]
+    spot = lax.axis_index("space")
+    place = jnp.stack([jnp.where(spot == 0, 2, 0), jnp.where(spot == slabs - 1, nz + 2, nz + 4)])
+    sums = jnp.pad(sums, (0, nx - sums.shape[0]))[None]
+    partial = local_moments(place.astype(jnp.int32), excess_phonon_enthalpy, table, sums, groups)
     reduced = lax.psum_scatter(partial, "mode", scatter_dimension=0, tiled=True)[0]
-    _, deep, ny, nx = reduced.shape
-    nz = deep - 4
-    part = nx // slabs
-    cut = reduced.reshape(8, deep, ny, slabs, part)
-    cut = jnp.transpose(cut, (3, 0, 1, 2, 4))
-    cut = lax.all_to_all(cut, "space", split_axis=0, concat_axis=0, tiled=True)
+    scalars = reduced[0, 0, 0]
+    slab = lax.all_gather(reduced, "space", axis=0)
     height = nz * slabs
     summed = None
     for s in range(slabs):
-        term = jnp.pad(cut[s], ((0, 0), (s * nz, height - (s + 1) * nz), (0, 0), (0, 0)))
+        term = slab[s]
+        term = jnp.concatenate([jnp.zeros_like(term[:1, :1]), term[:1, 1:]], axis=1)
+        term = jnp.concatenate([term, slab[s, 1:]], axis=0)
+        term = jnp.pad(term, ((0, 0), (s * nz, height - (s + 1) * nz), (0, 0), (0, 0)))
         summed = term if summed is None else summed + term
     summed = summed[:, 2:-2]
-    moments = widen(summed, sides, HALO)
-
-    def fill(values):
-        extra = -values.shape[-1] % 128
-        return jnp.pad(values, ((0, 0),) * (values.ndim - 1) + ((0, extra),))
-
-    temp, flux = heat(scalars, fill(moments), fill(start[0]), fill(start[1]))
-    rows = slice(HALO, HALO + ny)
-    columns = slice(HALO, HALO + part)
-    return (
-        jnp.transpose(temp[:, rows, columns], (2, 1, 0)),
-        jnp.transpose(flux[:, :, rows, columns], (0, 3, 2, 1)),
-    )
+    low, high = beside(summed, 2, HALO)
+    temp, flux = heat(scalars, summed, low, high, start[0], start[1])
+    part = nx // slabs
+    temp = lax.dynamic_slice_in_dim(temp, spot * part, part, axis=2)
+    flux = lax.dynamic_slice_in_dim(flux, spot * part, part, axis=3)
+    return jnp.transpose(temp, (2, 1, 0)), jnp.transpose(flux, (0, 3, 2, 1))
 
 
 def solution(mesh):

time: 288 us -> 224 us (0.78)
  the two profiles are of different devices: /device:TPU:14 before, /device:TPU:1 now
where the time goes in v2:
time: 224 us; the launch traced here: 222 us
  Pallas kernels  73.9 us (33%)
  waiting for transfers between devices  70.6 us (32%)
  blocking collectives  26.1 us (12%)
  local copies, waits for them, and re-layouts  14.9 us (7%)
  starting transfers between devices  14.6 us (7%)
  between operations  14.3 us (6%)
  other arithmetic  7.95 us (4%)
    pallas_call x1, Pallas kernels, local_moments(): pl.pallas_call(moments_kernel, grid=(nz, nx // width), in_specs=[pl.Block...  66.2 us
    reduce_scatter x1, waiting for transfers between devices, per_device(): lax.psum_scatter(partial, 'mode', scatter_dimension=0, tiled=True)[0]  55.2 us
    all_gather x1, blocking collectives, per_device(): lax.all_gather(start, 'space', axis=2, tiled=True)  26.1 us
    all_gather x1, waiting for transfers between devices, per_device(): slab = lax.all_gather(reduced, 'space', axis=0)  8.59 us
    ppermute x2, starting transfers between devices, beside(): lax.ppermute(tail, 'mode', [(i, i + 1) for i in range(ends)])  8.11 us
    pallas_call x1, Pallas kernels, heat(): pl.pallas_call(heat_kernel, in_specs=[pl.BlockSpec(memory_space=pltpu.SME...  7.7 us
    ppermute x2, starting transfers between devices, beside(): lax.ppermute(head, 'mode', [(i + 1, i) for i in range(ends)])  6.41 us
  transfers between devices with their start and end apart: 6, of which 4 were waited for; matrix products, arithmetic and copies ran while one was open for 5% of the time, Pallas kernels for 0%

profile of v2, /device:TPU:1, one launch (start us, length us, event | category | flops | bytes accessed | tf_op | source)
XLA Modules:
  0.0 222.5 jit_solution(4135055047428319756)
XLA Ops:
  7.2 0.0 reduce-scatter.2.cloned.1.call-start
  7.2 0.8 select_reduce_fusion
  8.0 0.7 fusion.8
  8.7 1.3 multiply_reduce_fusion.1
  10.0 0.7 fusion.7
  10.8 0.2 concatenate.42
  10.9 0.1 stack.180
  11.0 0.1 fusion.9
  11.2 0.1 multiply_reduce_fusion
  11.3 0.1 copy.22
  11.4 0.1 reshape.59
  11.5 0.7 pad_add_fusion.1.place_ref
  12.2 0.7 pad_maximum_fusion.1.a_ref
  12.9 1.2 fusion.4.sums_ref
  14.1 66.2 %moments.1 = f32[8,6,12,16,128]{4,3,2,1,0:T(8,128)} custom-call(s32[2]{0:T(128)} %pad_add_fusion.1.place_ref, bf16[96,8,128,128]{3,2,1,0:T(8,128)(2,1)} %e_ref.1, bf16[200,192]{1,0:T(8,128)(2,1)} %pad_maximum_fusion.1.a_ref, f32[1,128]{1,0:T(1,128)} %fusion.4.sums_ref), custom_call_target="tpu_custom_call" | custom-call | tf_op jit(solution)/shard_map/moments/pallas_call | solution.py:140
  80.4 0.0 reduce-scatter.2.cloned.1.call-update
  80.4 0.0 all-gather.2.cloned.1.call-start
  80.5 55.2 %reduce-scatter.2.cloned.1.call-done = f32[1,6,12,16,128]{4,3,2,1,0:T(8,128)} async-done(((f32[8,6,12,16,128]{4,3,2,1,0:T(8,128)}), f32[1,6,12,16,128]{4,3,2,1,0:T(8,128)}) %reduce-scatter.2.cloned.1.call-update) | async-done | bytes 589840 | tf_op jit(solution)/shard_map/reduce_scatter | solution.py:306
  135.6 0.0 all-gather.2.cloned.1.call-update
  135.8 26.1 %all_gather.7 = f32[2,32,128,16]{1,3,0,2:T(8,128)S(1)} all-gather(f32[2,32,32,16]{1,3,0,2:T(8,128)S(1)} %maximum_bitcast_fusion), channel_id=1, replica_groups=mesh['space'=4,'mode'=8] {'space'}, dimensions={2}, use_global_device_ids=true | all-gather | bytes 655360 | tf_op jit(solution)/shard_map/all_gather | solution.py:297
  161.9 1.4 copy.23
  163.3 0.7 fusion.12
  164.1 4.5 %collective-permute-start.3 = (f32[2,32,8,128]{3,2,1,0:T(8,128)}, f32[2,32,8,128]{3,2,1,0:T(8,128)}, u32[]{:S(2)}, u32[]{:S(2)}) collective-permute-start(f32[2,32,8,128]{3,2,1,0:T(8,128)} %get-tuple-element.41), channel_id=1, source_target_pairs={{1,0},{2,1},{3,2},{4,3},{5,4},{6,5},{7,6},{9,8},{10,9},{11,10},{12... | collective-permute-start | bytes 786440 | tf_op jit(solution)/shard_map/ppermute | solution.py:252
  168.6 4.3 %collective-permute-start.2 = (f32[2,32,8,128]{3,2,1,0:T(8,128)S(1)}, f32[2,32,8,128]{3,2,1,0:T(8,128)}, u32[]{:S(2)}, u32[]{:S(2)}) collective-permute-start(f32[2,32,8,128]{3,2,1,0:T(8,128)S(1)} %get-tuple-element.40), channel_id=1, source_target_pairs={{0,1},{1,2},{2,3},{3,4},{4,5},{5,6},{6,7},{8,9},{9,10},{10,11},{11... | collective-permute-start | bytes 786440 | tf_op jit(solution)/shard_map/ppermute | solution.py:251
  172.9 8.6 %all-gather.2.cloned.1.call-done = f32[4,6,12,16,128]{4,3,2,1,0:T(8,128)} async-done(((f32[1,6,12,16,128]{4,3,2,1,0:T(8,128)}), f32[4,6,12,16,128]{4,3,2,1,0:T(8,128)}) %all-gather.2.cloned.1.call-update) | async-done | bytes 2359312 | tf_op jit(solution)/shard_map/all_gather | solution.py:308
  181.5 1.9 slice_bitcast_fusion.3
  183.4 0.4 copy-done
  183.8 0.2 slice_bitcast_fusion.9
  184.0 0.1 select_maximum_fusion
  184.1 0.1 select_maximum_fusion.1
  184.1 0.1 select_maximum_fusion.2
  184.2 0.1 select_maximum_fusion.3
  184.3 0.2 pad_add_fusion
  184.4 1.3 fusion.11
  185.7 3.8 %collective-permute-start = (f32[6,32,8,128]{3,2,1,0:T(8,128)}, f32[6,32,8,128]{3,2,1,0:T(8,128)S(1)}, u32[]{:S(2)}, u32[]{:S(2)}) collective-permute-start(f32[6,32,8,128]{3,2,1,0:T(8,128)} %get-tuple-element.37), channel_id=1, source_target_pairs={{0,1},{1,2},{2,3},{3,4},{4,5},{5,6},{6,7},{8,9},{9,10},{10,11},{11... | collective-permute-start | bytes 2359304 | tf_op jit(solution)/shard_map/ppermute | solution.py:251
  189.6 1.9 collective-permute-start.1
  191.5 0.0 collective-permute-done.3
  191.5 1.1 pad_maximum_fusion
  192.6 1.1 slice_bitcast_fusion.4
  193.7 1.3 slice_bitcast_fusion.10.s_ref
  195.0 1.4 slice.95.m_ref
  196.3 2.4 %collective-permute-done.low_ref = f32[6,32,8,128]{3,2,1,0:T(8,128)S(1)} collective-permute-done((f32[6,32,8,128]{3,2,1,0:T(8,128)}, f32[6,32,8,128]{3,2,1,0:T(8,128)S(1)}, u32[]{:S(2)}, u32[]{:S(2)}) %collective-permute-start) | collective-permute-done | bytes 786464 | tf_op jit(solution)/shard_map/ppermute | solution.py:251
  198.8 4.4 %collective-permute-done.1.high_ref = f32[6,32,8,128]{3,2,1,0:T(8,128)} collective-permute-done((f32[6,32,8,128]{3,2,1,0:T(8,128)}, f32[6,32,8,128]{3,2,1,0:T(8,128)}, u32[]{:S(2)}, u32[]{:S(2)}) %collective-permute-start.1) | collective-permute-done | bytes 786464 | tf_op jit(solution)/shard_map/ppermute | solution.py:252
  203.2 7.7 %heat.1 = (f32[32,16,128]{2,1,0:T(8,128)}, f32[3,32,16,128]{3,2,1,0:T(8,128)}) custom-call(f32[128]{0:T(128)} %slice_bitcast_fusion.10.s_ref, f32[6,32,16,128]{3,2,1,0:T(8,128)} %slice.95.m_ref, f32[6,32,8,128]{3,2,1,0:T(8,128)} %copy-done.1, f32[6,32,8,128]{3,2,1,0:T(8,128)} %collective-permute-done.1.high_ref, f32[32,32,128]{2,1,0:T(8,128)} %get-tuple-element.39.t_ref, ...), custom_call_target="tpu_custom_call" | custom-call | tf_op jit(solution)/shard_map/heat/pallas_call | solution.py:232
  210.9 1.1 dynamic-slice_bitcast_fusion.1
  212.0 0.9 copy.24
  212.9 1.4 dynamic-slice_bitcast_fusion
  214.3 1.4 copy.25
  (23 shorter events, 0.2 us)
Async XLA Ops:
  7.2 128.5 %reduce-scatter.2.cloned.1.call-start = ((), (), s32[]{:S(2)}) async-start(), calls=%async_computation.1 | async-start | bytes 5308416 | tf_op jit(solution)/shard_map/reduce_scatter | solution.py:306
  80.4 55.3 %copy-start.2 = (f32[32,16,32]{2,1,0:T(8,128)S(1)}, f32[32,16,32]{2,1,0:T(8,128)}, u32[]{:S(2)}) copy-start(f32[32,16,32]{2,1,0:T(8,128)} %param.16) | copy-start | bytes 196612
  80.4 55.3 %copy-start.3 = (s32[32,16,32]{2,1,0:T(8,128)S(1)}, s32[32,16,32]{2,1,0:T(8,128)}, u32[]{:S(2)}) copy-start(s32[32,16,32]{2,1,0:T(8,128)} %param.17) | copy-start | bytes 196612
  80.4 55.3 %copy-start.4 = (f32[32,16,32]{2,1,0:T(8,128)S(1)}, f32[32,16,32]{2,1,0:T(8,128)}, u32[]{:S(2)}) copy-start(f32[32,16,32]{2,1,0:T(8,128)} %param.10) | copy-start | bytes 196612
  80.4 101.0 %all-gather.2.cloned.1.call-start = ((), (), s32[]{:S(2)}) async-start(), calls=%async_computation.2 | async-start | bytes 2949120 | tf_op jit(solution)/shard_map/all_gather | solution.py:308
  164.1 27.4 %collective-permute-start.3 = (f32[2,32,8,128]{3,2,1,0:T(8,128)}, f32[2,32,8,128]{3,2,1,0:T(8,128)}, u32[]{:S(2)}, u32[]{:S(2)}) collective-permute-start(f32[2,32,8,128]{3,2,1,0:T(8,128)} %get-tuple-element.41), channel_id=1, source_target_pairs={{1,0},{2,1},{3,2},{4,3},{5,4},{6,5},{7,6},{9,8},{10,9},{11,10},{12... | collective-permute-start | bytes 786440 | tf_op jit(solution)/shard_map/ppermute | solution.py:252
  168.6 22.9 %collective-permute-start.2 = (f32[2,32,8,128]{3,2,1,0:T(8,128)S(1)}, f32[2,32,8,128]{3,2,1,0:T(8,128)}, u32[]{:S(2)}, u32[]{:S(2)}) collective-permute-start(f32[2,32,8,128]{3,2,1,0:T(8,128)S(1)} %get-tuple-element.40), channel_id=1, source_target_pairs={{0,1},{1,2},{2,3},{3,4},{4,5},{5,6},{6,7},{8,9},{9,10},{10,11},{11... | collective-permute-start | bytes 786440 | tf_op jit(solution)/shard_map/ppermute | solution.py:251
  181.5 2.4 %copy-start = (f32[4,6,12,16,128]{4,3,2,1,0:T(8,128)S(1)}, f32[4,6,12,16,128]{4,3,2,1,0:T(8,128)}, u32[]{:S(2)}) copy-start(f32[4,6,12,16,128]{4,3,2,1,0:T(8,128)} %all-gather.2.cloned.1.call-done) | copy-start | bytes 7077892
  185.7 13.1 %collective-permute-start = (f32[6,32,8,128]{3,2,1,0:T(8,128)}, f32[6,32,8,128]{3,2,1,0:T(8,128)S(1)}, u32[]{:S(2)}, u32[]{:S(2)}) collective-permute-start(f32[6,32,8,128]{3,2,1,0:T(8,128)} %get-tuple-element.37), channel_id=1, source_target_pairs={{0,1},{1,2},{2,3},{3,4},{4,5},{5,6},{6,7},{8,9},{9,10},{10,11},{11... | collective-permute-start | bytes 2359304 | tf_op jit(solution)/shard_map/ppermute | solution.py:251
  189.6 13.6 %collective-permute-start.1 = (f32[6,32,8,128]{3,2,1,0:T(8,128)}, f32[6,32,8,128]{3,2,1,0:T(8,128)}, u32[]{:S(2)}, u32[]{:S(2)}) collective-permute-start(f32[6,32,8,128]{3,2,1,0:T(8,128)} %get-tuple-element.36), channel_id=1, source_target_pairs={{1,0},{2,1},{3,2},{4,3},{5,4},{6,5},{7,6},{9,8},{10,9},{11,10},{12... | collective-permute-start | bytes 2359304 | tf_op jit(solution)/shard_map/ppermute | solution.py:252
  198.8 4.4 %copy-start.1 = (f32[6,32,8,128]{3,2,1,0:T(8,128)}, f32[6,32,8,128]{3,2,1,0:T(8,128)S(1)}, u32[]{:S(2)}) copy-start(f32[6,32,8,128]{3,2,1,0:T(8,128)S(1)} %collective-permute-done.low_ref) | copy-start | bytes 2359300
Sparse Core Ops, SparseCore 0:
  80.5 55.0 reduce-scatter.1
  137.5 43.9 all-gather.1

commit v3 on v2

--- a/solution.py
+++ b/solution.py
@@ -58,7 +58,7 @@
     width = e_ref.shape[2]
     lanes = e_ref.shape[3]
     planes = mid.shape[0]
-    across = mid.shape[1] - 4
+    across = mid.shape[1] // 8 - 4
 
     @pl.when((z == 0) & (xb == 0))
     def _():
@@ -86,7 +86,7 @@
                 elif dy == -2:
                     part = jnp.where(lane < lanes - 2, pltpu.roll(part, lanes - 2, 1), 0.0)
                 ref = {1: plus, -1: minus}.get(dy, mid)
-                ref[z + (2 + dz), x + (2 + dx)] += part
+                ref[z + (2 + dz), pl.ds(pl.multiple_of(8 * (x + (2 + dx)), 8), 8), :] += part
 
     @pl.when((z == pl.num_programs(0) - 1) & (xb == pl.num_programs(1) - 1))
     def _():
@@ -110,9 +110,9 @@
         def finish(p, below):
             upright = []
             for k in range(8):
-                up = pltpu.roll(plus[p, pl.ds(2, across), k, :], 1, 1)
-                down = pltpu.roll(minus[p, pl.ds(2, across), k, :], lanes - 1, 1)
-                whole = mid[p, pl.ds(2, across), k, :]
+                up = pltpu.roll(plus[p, pl.ds(16 + k, across, stride=8), :], 1, 1)
+                down = pltpu.roll(minus[p, pl.ds(16 + k, across, stride=8), :], lanes - 1, 1)
+                whole = mid[p, pl.ds(16 + k, across, stride=8), :]
                 whole = whole + jnp.where(spot >= 1, up, 0.0)
                 whole = whole + jnp.where(spot < lanes - 1, down, 0.0)
                 upright.append(whole.T)
@@ -135,7 +135,7 @@
 def local_moments(place, state, table, sums, blocks):
     modes, nz, nx, ny = state.shape
     width = math.gcd(nx, 16)
-    acc = pltpu.VMEM((nz + 4, nx + 4, 8, ny), jnp.float32)
+    acc = pltpu.VMEM((nz + 4, 8 * (nx + 4), ny), jnp.float32)
     shape = (blocks, 6, nz + 4, ny // blocks, nx)
     return pl.pallas_call(
         moments_kernel,
@@ -149,6 +149,11 @@
         out_specs=pl.BlockSpec(shape, lambda z, x: (0, 0, 0, 0, 0)),
         out_shape=jax.ShapeDtypeStruct(shape, jnp.float32),
         scratch_shapes=[acc, acc, acc],
+        cost_estimate=pl.CostEstimate(
+            flops=2 * table.shape[0] * table.shape[1] * nz * nx * ny,
+            bytes_accessed=2 * state.size,
+            transcendentals=0,
+        ),
         compiler_params=pltpu.CompilerParams(
             dimension_semantics=("arbitrary", "arbitrary"), vmem_limit_bytes=60 * 1024 * 1024
         ),
@@ -293,8 +298,9 @@
     table = jnp.concatenate([high, table - high], axis=1).astype(jnp.bfloat16)
 
     kappa = thermal_conductance_bulk * jnp.where(substance_label == 1, pore_factor, 1.0)
-    start = jnp.transpose(jnp.stack([thermal_offset, kappa]), (0, 3, 1, 2))
-    start = jnp.transpose(lax.all_gather(start, "space", axis=2, tiled=True), (0, 1, 3, 2))
+    start = jnp.transpose(jnp.stack([thermal_offset, kappa]), (0, 3, 2, 1))
+    start = lax.all_gather(start, "space", axis=0)
+    start = jnp.concatenate([start[s] for s in range(slabs)], axis=3)
     low, high = beside(start, 2, HALO)
     start = jnp.concatenate([low, start, high], axis=2)
 
@@ -304,15 +310,14 @@
     sums = jnp.pad(sums, (0, nx - sums.shape[0]))[None]
     partial = local_moments(place.astype(jnp.int32), excess_phonon_enthalpy, table, sums, groups)
     reduced = lax.psum_scatter(partial, "mode", scatter_dimension=0, tiled=True)[0]
-    scalars = reduced[0, 0, 0]
+    reduced, start = lax.optimization_barrier((reduced, start))
+    scalars, reduced = lax.optimization_barrier((reduced[0, 0, 0], reduced))
+    reduced = reduced.at[0, 0].set(0.0)
     slab = lax.all_gather(reduced, "space", axis=0)
     height = nz * slabs
     summed = None
     for s in range(slabs):
-        term = slab[s]
-        term = jnp.concatenate([jnp.zeros_like(term[:1, :1]), term[:1, 1:]], axis=1)
-        term = jnp.concatenate([term, slab[s, 1:]], axis=0)
-        term = jnp.pad(term, ((0, 0), (s * nz, height - (s + 1) * nz), (0, 0), (0, 0)))
+        term = jnp.pad(slab[s], ((0, 0), (s * nz, height - (s + 1) * nz), (0, 0), (0, 0)))
         summed = term if summed is None else summed + term
     summed = summed[:, 2:-2]
     low, high = beside(summed, 2, HALO)

time: 224 us -> 213 us (0.951)
  Pallas kernels: 73.9 us -> 68.7 us
  blocking collectives: 26.1 us -> 21.4 us
  waiting for transfers between devices: 70.6 us -> 73.7 us
    reduce_scatter x1, waiting for transfers between devices: 55.2 us -> 14.3 us  [per_device(): lax.psum_scatter(partial, 'mode', scatter_dimension=0, tiled=True)[0]]
    all_gather x1, waiting for transfers between devices: 8.59 us -> 37.7 us  [per_device(): slab = lax.all_gather(reduced, 'space', axis=0)]
    ppermute x2, waiting for transfers between devices: 2.45 us -> 12 us  [beside(): lax.ppermute(tail, 'mode', [(i, i + 1) for i in range(ends)])]
    ppermute x2, waiting for transfers between devices: 4.4 us -> 9.7 us  [beside(): lax.ppermute(head, 'mode', [(i + 1, i) for i in range(ends)])]
    pallas_call x1, Pallas kernels: 66.2 us -> 61 us  [local_moments(): pl.pallas_call(moments_kernel, grid=(nz, nx // width), in_specs=[pl.Block...]
    all_gather x1, blocking collectives: 26.1 us -> 21.4 us  [per_device(): start = lax.all_gather(start, 'space', axis=0)]
    ppermute x2, starting transfers between devices: 6.41 us -> 3.84 us  [beside(): lax.ppermute(head, 'mode', [(i + 1, i) for i in range(ends)])]
  transfers between devices with their start and end apart: 6 -> 6, of which waited for: 4 -> 6; matrix products, arithmetic and copies ran while one was open for 5% -> 2% of each run, Pallas kernels for 0% -> 0%
where the time goes in v3:
time: 213 us; the launch traced here: 212 us
  waiting for transfers between devices  73.7 us (35%)
  Pallas kernels  68.7 us (32%)
  blocking collectives  21.4 us (10%)
  between operations  14.2 us (7%)
  local copies, waits for them, and re-layouts  13.1 us (6%)
  starting transfers between devices  13 us (6%)
  other arithmetic  7.48 us (4%)
    pallas_call x1, Pallas kernels, local_moments(): pl.pallas_call(moments_kernel, grid=(nz, nx // width), in_specs=[pl.Block...  61 us
    all_gather x1, waiting for transfers between devices, per_device(): slab = lax.all_gather(reduced, 'space', axis=0)  37.7 us
    all_gather x1, blocking collectives, per_device(): start = lax.all_gather(start, 'space', axis=0)  21.4 us
    reduce_scatter x1, waiting for transfers between devices, per_device(): lax.psum_scatter(partial, 'mode', scatter_dimension=0, tiled=True)[0]  14.3 us
    ppermute x2, waiting for transfers between devices, beside(): lax.ppermute(tail, 'mode', [(i, i + 1) for i in range(ends)])  12 us
    ppermute x2, waiting for transfers between devices, beside(): lax.ppermute(head, 'mode', [(i + 1, i) for i in range(ends)])  9.7 us
    ppermute x2, starting transfers between devices, beside(): lax.ppermute(tail, 'mode', [(i, i + 1) for i in range(ends)])  9.03 us
    pallas_call x1, Pallas kernels, heat(): pl.pallas_call(heat_kernel, in_specs=[pl.BlockSpec(memory_space=pltpu.SME...  7.7 us
  transfers between devices with their start and end apart: 6, of which 6 were waited for; matrix products, arithmetic and copies ran while one was open for 2% of the time, Pallas kernels for 0%

profile of v3, /device:TPU:1, one launch (start us, length us, event | category | flops | bytes accessed | tf_op | source)
XLA Modules:
  0.0 211.6 jit_solution(16999698760492296666)
XLA Ops:
  7.2 0.0 reduce-scatter.2.cloned.1.call-start
  7.2 0.8 select_reduce_fusion
  8.0 0.7 fusion.8
  8.7 1.4 multiply_reduce_fusion.1
  10.1 0.7 fusion.7
  10.8 0.2 concatenate.23
  11.0 0.1 stack.180
  11.1 0.1 fusion.9
  11.3 0.1 multiply_reduce_fusion
  11.3 0.1 copy.24
  11.4 0.1 reshape.96
  11.5 0.7 pad_maximum_fusion.2.a_ref
  12.3 0.6 pad_add_fusion.1.place_ref
  12.8 1.2 fusion.4.sums_ref
  14.0 61.0 %moments.1 = f32[8,6,12,16,128]{4,3,2,1,0:T(8,128)} custom-call(s32[2]{0:T(128)} %pad_add_fusion.1.place_ref, bf16[96,8,128,128]{3,2,1,0:T(8,128)(2,1)} %e_ref.1, bf16[200,192]{1,0:T(8,128)(2,1)} %pad_maximum_fusion.2.a_ref, f32[1,128]{1,0:T(1,128)} %fusion.4.sums_ref), custom_call_target="tpu_custom_call" | custom-call | flops 10066329600 | bytes 25165824 | tf_op jit(solution)/shard_map/moments/pallas_call | solution.py:140
  75.1 0.0 reduce-scatter.2.cloned.1.call-update
  75.1 0.0 all-gather.3.cloned.1.call-start
  75.2 0.9 copy-done.1
  76.0 0.2 copy.26
  76.2 0.2 copy.27
  76.4 0.2 copy.25
  76.7 21.4 %all-gather = f32[8,32,16,32]{3,2,1,0:T(8,128)S(1)} all-gather(f32[2,32,16,32]{3,2,1,0:T(8,128)S(1)} %maximum_bitcast_fusion), channel_id=2, replica_groups=mesh['space'=4,'mode'=8] {'space'}, dimensions={0}, use_global_device_ids=true | all-gather | bytes 655360 | tf_op jit(solution)/shard_map/all_gather | solution.py:302
  98.1 0.1 fusion.11
  98.3 0.5 pad_maximum_fusion.1
  98.8 5.2 %collective-permute-start = (f32[2,32,8,128]{3,2,1,0:T(8,128)S(1)}, f32[2,32,8,128]{3,2,1,0:T(8,128)S(1)}, u32[]{:S(2)}, u32[]{:S(2)}) collective-permute-start(f32[2,32,8,128]{3,2,1,0:T(8,128)S(1)} %get-tuple-element.60), channel_id=1, source_target_pairs={{0,1},{1,2},{2,3},{3,4},{4,5},{5,6},{6,7},{8,9},{9,10},{10,11},{11... | collective-permute-start | bytes 786440 | tf_op jit(solution)/shard_map/ppermute | solution.py:256
  104.0 1.9 collective-permute-start.1
  105.9 7.1 %collective-permute-done = f32[2,32,8,128]{3,2,1,0:T(8,128)S(1)} collective-permute-done((f32[2,32,8,128]{3,2,1,0:T(8,128)S(1)}, f32[2,32,8,128]{3,2,1,0:T(8,128)S(1)}, u32[]{:S(2)}, u32[]{:S(2)}) %collective-permute-start) | collective-permute-done | bytes 262176 | tf_op jit(solution)/shard_map/ppermute | solution.py:256
  113.1 5.3 %collective-permute-done.1 = f32[2,32,8,128]{3,2,1,0:T(8,128)S(1)} collective-permute-done((f32[2,32,8,128]{3,2,1,0:T(8,128)S(1)}, f32[2,32,8,128]{3,2,1,0:T(8,128)S(1)}, u32[]{:S(2)}, u32[]{:S(2)}) %collective-permute-start.1) | collective-permute-done | bytes 262176 | tf_op jit(solution)/shard_map/ppermute | solution.py:257
  118.4 0.5 pad_maximum_fusion
  118.8 14.3 %reduce-scatter.2.cloned.1.call-done = f32[1,6,12,16,128]{4,3,2,1,0:T(8,128)} async-done(((f32[8,6,12,16,128]{4,3,2,1,0:T(8,128)}), f32[1,6,12,16,128]{4,3,2,1,0:T(8,128)}) %reduce-scatter.2.cloned.1.call-update) | async-done | bytes 589840 | tf_op jit(solution)/shard_map/reduce_scatter | solution.py:312
  133.1 1.2 slice_bitcast_fusion.6.s_ref
  134.3 0.6 broadcast_dynamic-update-slice_fusion
  134.9 0.0 all-gather.3.cloned.1.call-update
  134.9 37.7 %all-gather.3.cloned.1.call-done = f32[4,6,12,16,128]{4,3,2,1,0:T(8,128)} async-done(((f32[1,6,12,16,128]{4,3,2,1,0:T(8,128)}), f32[4,6,12,16,128]{4,3,2,1,0:T(8,128)}) %all-gather.3.cloned.1.call-update) | async-done | bytes 2359312 | tf_op jit(solution)/shard_map/all_gather | solution.py:316
  172.6 1.8 slice_bitcast_fusion.3
  174.3 0.2 pad_add_fusion
  174.5 1.3 fusion.12
  175.8 3.8 %collective-permute-start.2 = (f32[6,32,8,128]{3,2,1,0:T(8,128)}, f32[6,32,8,128]{3,2,1,0:T(8,128)}, u32[]{:S(2)}, u32[]{:S(2)}) collective-permute-start(f32[6,32,8,128]{3,2,1,0:T(8,128)} %get-tuple-element.57), channel_id=1, source_target_pairs={{0,1},{1,2},{2,3},{3,4},{4,5},{5,6},{6,7},{8,9},{9,10},{10,11},{11... | collective-permute-start | bytes 2359304 | tf_op jit(solution)/shard_map/ppermute | solution.py:256
  179.6 1.9 collective-permute-start.3
  181.6 1.0 slice_bitcast_fusion.4
  182.6 1.3 slice.107.m_ref
  183.9 4.9 %collective-permute-done.2.low_ref = f32[6,32,8,128]{3,2,1,0:T(8,128)} collective-permute-done((f32[6,32,8,128]{3,2,1,0:T(8,128)}, f32[6,32,8,128]{3,2,1,0:T(8,128)}, u32[]{:S(2)}, u32[]{:S(2)}) %collective-permute-start.2) | collective-permute-done | bytes 786464 | tf_op jit(solution)/shard_map/ppermute | solution.py:256
  188.9 4.4 %collective-permute-done.3.high_ref = f32[6,32,8,128]{3,2,1,0:T(8,128)} collective-permute-done((f32[6,32,8,128]{3,2,1,0:T(8,128)}, f32[6,32,8,128]{3,2,1,0:T(8,128)}, u32[]{:S(2)}, u32[]{:S(2)}) %collective-permute-start.3) | collective-permute-done | bytes 786464 | tf_op jit(solution)/shard_map/ppermute | solution.py:257
  193.3 7.7 %heat.1 = (f32[32,16,128]{2,1,0:T(8,128)}, f32[3,32,16,128]{3,2,1,0:T(8,128)}) custom-call(f32[128]{0:T(128)} %slice_bitcast_fusion.6.s_ref, f32[6,32,16,128]{3,2,1,0:T(8,128)} %slice.107.m_ref, f32[6,32,8,128]{3,2,1,0:T(8,128)} %collective-permute-done.2.low_ref, f32[6,32,8,128]{3,2,1,0:T(8,128)} %collective-permute-done.3.high_ref, ...), custom_call_target="tpu_custom_call" | custom-call | tf_op jit(solution)/shard_map/heat/pallas_call | solution.py:237
  201.0 1.4 dynamic-slice_bitcast_fusion
  202.4 1.4 copy.29
  203.8 0.1 dynamic-slice_bitcast_fusion.1
  203.9 0.9 copy.28
  (17 shorter events, 0.2 us)
Async XLA Ops:
  7.2 126.0 %reduce-scatter.2.cloned.1.call-start = ((), (), s32[]{:S(2)}) async-start(), calls=%async_computation.1 | async-start | bytes 5308416 | tf_op jit(solution)/shard_map/reduce_scatter | solution.py:312
  75.1 0.9 copy-start.1
  75.1 1.1 copy-start.2
  75.1 1.4 copy-start.3
  75.1 97.5 %all-gather.3.cloned.1.call-start = ((), (), s32[]{:S(2)}) async-start(), calls=%async_computation.2 | async-start | bytes 2949120 | tf_op jit(solution)/shard_map/all_gather | solution.py:316
  98.8 14.2 %collective-permute-start = (f32[2,32,8,128]{3,2,1,0:T(8,128)S(1)}, f32[2,32,8,128]{3,2,1,0:T(8,128)S(1)}, u32[]{:S(2)}, u32[]{:S(2)}) collective-permute-start(f32[2,32,8,128]{3,2,1,0:T(8,128)S(1)} %get-tuple-element.60), channel_id=1, source_target_pairs={{0,1},{1,2},{2,3},{3,4},{4,5},{5,6},{6,7},{8,9},{9,10},{10,11},{11... | collective-permute-start | bytes 786440 | tf_op jit(solution)/shard_map/ppermute | solution.py:256
  104.0 14.3 %collective-permute-start.1 = (f32[2,32,8,128]{3,2,1,0:T(8,128)S(1)}, f32[2,32,8,128]{3,2,1,0:T(8,128)S(1)}, u32[]{:S(2)}, u32[]{:S(2)}) collective-permute-start(f32[2,32,8,128]{3,2,1,0:T(8,128)S(1)} %get-tuple-element.61), channel_id=1, source_target_pairs={{1,0},{2,1},{3,2},{4,3},{5,4},{6,5},{7,6},{9,8},{10,9},{11,10},{12... | collective-permute-start | bytes 786440 | tf_op jit(solution)/shard_map/ppermute | solution.py:257
  175.8 13.1 %collective-permute-start.2 = (f32[6,32,8,128]{3,2,1,0:T(8,128)}, f32[6,32,8,128]{3,2,1,0:T(8,128)}, u32[]{:S(2)}, u32[]{:S(2)}) collective-permute-start(f32[6,32,8,128]{3,2,1,0:T(8,128)} %get-tuple-element.57), channel_id=1, source_target_pairs={{0,1},{1,2},{2,3},{3,4},{4,5},{5,6},{6,7},{8,9},{9,10},{10,11},{11... | collective-permute-start | bytes 2359304 | tf_op jit(solution)/shard_map/ppermute | solution.py:256
  179.6 13.6 %collective-permute-start.3 = (f32[6,32,8,128]{3,2,1,0:T(8,128)}, f32[6,32,8,128]{3,2,1,0:T(8,128)}, u32[]{:S(2)}, u32[]{:S(2)}) collective-permute-start(f32[6,32,8,128]{3,2,1,0:T(8,128)} %get-tuple-element.56), channel_id=1, source_target_pairs={{1,0},{2,1},{3,2},{4,3},{5,4},{6,5},{7,6},{9,8},{10,9},{11,10},{12... | collective-permute-start | bytes 2359304 | tf_op jit(solution)/shard_map/ppermute | solution.py:257
  201.0 2.8 %copy-start = (f32[32,16,128]{2,1,0:T(8,128)S(1)}, f32[32,16,128]{2,1,0:T(8,128)}, u32[]{:S(2)}) copy-start(f32[32,16,128]{2,1,0:T(8,128)} %get-tuple-element.24) | copy-start | bytes 786436
Sparse Core Ops, SparseCore 0:
  75.2 57.8 reduce-scatter.1
  135.0 37.4 all-gather.2

commit v4 on v3

--- a/solution.py
+++ b/solution.py
@@ -134,7 +134,7 @@
 
 def local_moments(place, state, table, sums, blocks):
     modes, nz, nx, ny = state.shape
-    width = math.gcd(nx, 16)
+    width = math.gcd(nx, 32)
     acc = pltpu.VMEM((nz + 4, 8 * (nx + 4), ny), jnp.float32)
     shape = (blocks, 6, nz + 4, ny // blocks, nx)
     return pl.pallas_call(
@@ -313,11 +313,11 @@
     reduced, start = lax.optimization_barrier((reduced, start))
     scalars, reduced = lax.optimization_barrier((reduced[0, 0, 0], reduced))
     reduced = reduced.at[0, 0].set(0.0)
-    slab = lax.all_gather(reduced, "space", axis=0)
+    slab = lax.all_gather(reduced.astype(jnp.bfloat16), "space", axis=0)
     height = nz * slabs
     summed = None
     for s in range(slabs):
-        term = jnp.pad(slab[s], ((0, 0), (s * nz, height - (s + 1) * nz), (0, 0), (0, 0)))
+        term = jnp.pad(slab[s].astype(jnp.float32), ((0, 0), (s * nz, height - (s + 1) * nz), (0, 0), (0, 0)))
         summed = term if summed is None else summed + term
     summed = summed[:, 2:-2]
     low, high = beside(summed, 2, HALO)

time: 213 us -> 186 us (0.87)
  Pallas kernels: 68.7 us -> 50.3 us
  waiting for transfers between devices: 73.7 us -> 64 us
    pallas_call x1, Pallas kernels: 61 us -> 42.6 us  [local_moments(): pl.pallas_call(moments_kernel, grid=(nz, nx // width), in_specs=[pl.Block...]
    all_gather x1, waiting for transfers between devices: 37.7 us -> 27.9 us  [per_device(): slab = lax.all_gather(reduced.astype(jnp.bfloat16), 'space', axis=0)]
where the time goes in v4:
time: 186 us; the launch traced here: 185 us
  waiting for transfers between devices  64 us (34%)
  Pallas kernels  50.3 us (27%)
  blocking collectives  21.4 us (12%)
  between operations  14.2 us (8%)
  starting transfers between devices  13 us (7%)
  local copies, waits for them, and re-layouts  12.8 us (7%)
  other arithmetic  9.3 us (5%)
    pallas_call x1, Pallas kernels, local_moments(): pl.pallas_call(moments_kernel, grid=(nz, nx // width), in_specs=[pl.Block...  42.6 us
    all_gather x1, waiting for transfers between devices, per_device(): slab = lax.all_gather(reduced.astype(jnp.bfloat16), 'space', axis=0)  27.9 us
    all_gather x1, blocking collectives, per_device(): start = lax.all_gather(start, 'space', axis=0)  21.4 us
    reduce_scatter x1, waiting for transfers between devices, per_device(): lax.psum_scatter(partial, 'mode', scatter_dimension=0, tiled=True)[0]  14.3 us
    ppermute x2, waiting for transfers between devices, beside(): lax.ppermute(tail, 'mode', [(i, i + 1) for i in range(ends)])  12 us
    ppermute x2, waiting for transfers between devices, beside(): lax.ppermute(head, 'mode', [(i + 1, i) for i in range(ends)])  9.71 us
    ppermute x2, starting transfers between devices, beside(): lax.ppermute(tail, 'mode', [(i, i + 1) for i in range(ends)])  9.03 us
    pallas_call x1, Pallas kernels, heat(): pl.pallas_call(heat_kernel, in_specs=[pl.BlockSpec(memory_space=pltpu.SME...  7.7 us
  transfers between devices with their start and end apart: 6, of which 6 were waited for; matrix products, arithmetic and copies ran while one was open for 2% of the time, Pallas kernels for 0%

profile of v4, /device:TPU:1, one launch (start us, length us, event | category | flops | bytes accessed | tf_op | source)
XLA Modules:
  0.0 184.9 jit_solution(16204901289376430719)
XLA Ops:
  7.2 0.0 reduce-scatter.2.cloned.1.call-start
  7.2 0.8 select_reduce_fusion
  8.0 0.7 fusion.8
  8.7 1.4 multiply_reduce_fusion.1
  10.1 0.7 fusion.7
  10.8 0.2 concatenate.23
  11.0 0.1 stack.180
  11.1 0.1 fusion.9
  11.3 0.1 multiply_reduce_fusion
  11.3 0.1 copy.24
  11.4 0.1 reshape.102
  11.5 0.7 pad_maximum_fusion.2.a_ref
  12.3 0.6 pad_add_fusion.place_ref
  12.8 1.2 fusion.4.sums_ref
  14.0 42.6 %moments.1 = f32[8,6,12,16,128]{4,3,2,1,0:T(8,128)} custom-call(s32[2]{0:T(128)} %pad_add_fusion.place_ref, bf16[96,8,128,128]{3,2,1,0:T(8,128)(2,1)} %e_ref.1, bf16[200,192]{1,0:T(8,128)(2,1)} %pad_maximum_fusion.2.a_ref, f32[1,128]{1,0:T(1,128)} %fusion.4.sums_ref), custom_call_target="tpu_custom_call" | custom-call | flops 10066329600 | bytes 25165824 | tf_op jit(solution)/shard_map/moments/pallas_call | solution.py:140
  56.6 0.0 reduce-scatter.2.cloned.1.call-update
  56.6 0.0 all-gather.4.cloned.1.call-start
  56.7 0.9 copy-done.1
  57.6 0.2 copy.26
  57.8 0.2 copy.27
  58.0 0.2 copy.25
  58.3 21.4 %all-gather = f32[8,32,16,32]{3,2,1,0:T(8,128)S(1)} all-gather(f32[2,32,16,32]{3,2,1,0:T(8,128)S(1)} %maximum_bitcast_fusion), channel_id=2, replica_groups=mesh['space'=4,'mode'=8] {'space'}, dimensions={0}, use_global_device_ids=true | all-gather | bytes 655360 | tf_op jit(solution)/shard_map/all_gather | solution.py:302
  79.7 0.1 fusion.11
  79.8 0.5 pad_maximum_fusion.1
  80.3 5.2 %collective-permute-start = (f32[2,32,8,128]{3,2,1,0:T(8,128)S(1)}, f32[2,32,8,128]{3,2,1,0:T(8,128)S(1)}, u32[]{:S(2)}, u32[]{:S(2)}) collective-permute-start(f32[2,32,8,128]{3,2,1,0:T(8,128)S(1)} %get-tuple-element.60), channel_id=1, source_target_pairs={{0,1},{1,2},{2,3},{3,4},{4,5},{5,6},{6,7},{8,9},{9,10},{10,11},{11... | collective-permute-start | bytes 786440 | tf_op jit(solution)/shard_map/ppermute | solution.py:256
  85.6 1.9 %collective-permute-start.1 = (f32[2,32,8,128]{3,2,1,0:T(8,128)S(1)}, f32[2,32,8,128]{3,2,1,0:T(8,128)S(1)}, u32[]{:S(2)}, u32[]{:S(2)}) collective-permute-start(f32[2,32,8,128]{3,2,1,0:T(8,128)S(1)} %get-tuple-element.61), channel_id=1, source_target_pairs={{1,0},{2,1},{3,2},{4,3},{5,4},{6,5},{7,6},{9,8},{10,9},{11,10},{12... | collective-permute-start | bytes 786440 | tf_op jit(solution)/shard_map/ppermute | solution.py:257
  87.5 7.1 %collective-permute-done = f32[2,32,8,128]{3,2,1,0:T(8,128)S(1)} collective-permute-done((f32[2,32,8,128]{3,2,1,0:T(8,128)S(1)}, f32[2,32,8,128]{3,2,1,0:T(8,128)S(1)}, u32[]{:S(2)}, u32[]{:S(2)}) %collective-permute-start) | collective-permute-done | bytes 262176 | tf_op jit(solution)/shard_map/ppermute | solution.py:256
  94.6 5.3 %collective-permute-done.1 = f32[2,32,8,128]{3,2,1,0:T(8,128)S(1)} collective-permute-done((f32[2,32,8,128]{3,2,1,0:T(8,128)S(1)}, f32[2,32,8,128]{3,2,1,0:T(8,128)S(1)}, u32[]{:S(2)}, u32[]{:S(2)}) %collective-permute-start.1) | collective-permute-done | bytes 262176 | tf_op jit(solution)/shard_map/ppermute | solution.py:257
  99.9 0.5 pad_maximum_fusion
  100.4 14.3 %reduce-scatter.2.cloned.1.call-done = f32[1,6,12,16,128]{4,3,2,1,0:T(8,128)} async-done(((f32[8,6,12,16,128]{4,3,2,1,0:T(8,128)}), f32[1,6,12,16,128]{4,3,2,1,0:T(8,128)}) %reduce-scatter.2.cloned.1.call-update) | async-done | bytes 589840 | tf_op jit(solution)/shard_map/reduce_scatter | solution.py:312
  114.7 1.2 slice_bitcast_fusion.2.s_ref
  115.8 0.6 broadcast_dynamic-update-slice_fusion
  116.4 1.8 convert_element_type.39
  118.3 27.9 %all-gather.4.cloned.1.call-done = bf16[24,12,16,128]{3,2,1,0:T(8,128)(2,1)} async-done(((bf16[6,12,16,128]{3,2,1,0:T(8,128)(2,1)}), bf16[24,12,16,128]{3,2,1,0:T(8,128)(2,1)}) %all-gather.4.cloned.1.call-update) | async-done | bytes 1179664 | tf_op jit(solution)/shard_map/all_gather | solution.py:316
  146.2 1.4 fusion.13
  147.6 0.2 convert_add_fusion
  147.8 1.3 fusion.12
  149.1 3.8 %collective-permute-start.2 = (f32[6,32,8,128]{3,2,1,0:T(8,128)}, f32[6,32,8,128]{3,2,1,0:T(8,128)}, u32[]{:S(2)}, u32[]{:S(2)}) collective-permute-start(f32[6,32,8,128]{3,2,1,0:T(8,128)} %get-tuple-element.53), channel_id=1, source_target_pairs={{0,1},{1,2},{2,3},{3,4},{4,5},{5,6},{6,7},{8,9},{9,10},{10,11},{11... | collective-permute-start | bytes 2359304 | tf_op jit(solution)/shard_map/ppermute | solution.py:256
  152.9 1.9 %collective-permute-start.3 = (f32[6,32,8,128]{3,2,1,0:T(8,128)}, f32[6,32,8,128]{3,2,1,0:T(8,128)}, u32[]{:S(2)}, u32[]{:S(2)}) collective-permute-start(f32[6,32,8,128]{3,2,1,0:T(8,128)} %get-tuple-element.52), channel_id=1, source_target_pairs={{1,0},{2,1},{3,2},{4,3},{5,4},{6,5},{7,6},{9,8},{10,9},{11,10},{12... | collective-permute-start | bytes 2359304 | tf_op jit(solution)/shard_map/ppermute | solution.py:257
  154.9 1.0 slice_bitcast_fusion
  155.9 1.3 slice.111.m_ref
  157.2 4.9 %collective-permute-done.2.low_ref = f32[6,32,8,128]{3,2,1,0:T(8,128)} collective-permute-done((f32[6,32,8,128]{3,2,1,0:T(8,128)}, f32[6,32,8,128]{3,2,1,0:T(8,128)}, u32[]{:S(2)}, u32[]{:S(2)}) %collective-permute-start.2) | collective-permute-done | bytes 786464 | tf_op jit(solution)/shard_map/ppermute | solution.py:256
  162.2 4.4 %collective-permute-done.3.high_ref = f32[6,32,8,128]{3,2,1,0:T(8,128)} collective-permute-done((f32[6,32,8,128]{3,2,1,0:T(8,128)}, f32[6,32,8,128]{3,2,1,0:T(8,128)}, u32[]{:S(2)}, u32[]{:S(2)}) %collective-permute-start.3) | collective-permute-done | bytes 786464 | tf_op jit(solution)/shard_map/ppermute | solution.py:257
  166.6 7.7 %heat.1 = (f32[32,16,128]{2,1,0:T(8,128)}, f32[3,32,16,128]{3,2,1,0:T(8,128)}) custom-call(f32[128]{0:T(128)} %slice_bitcast_fusion.2.s_ref, f32[6,32,16,128]{3,2,1,0:T(8,128)} %slice.111.m_ref, f32[6,32,8,128]{3,2,1,0:T(8,128)} %collective-permute-done.2.low_ref, f32[6,32,8,128]{3,2,1,0:T(8,128)} %collective-permute-done.3.high_ref, ...), custom_call_target="tpu_custom_call" | custom-call | tf_op jit(solution)/shard_map/heat/pallas_call | solution.py:237
  174.3 1.4 dynamic-slice_bitcast_fusion
  175.7 1.4 copy.29
  177.1 0.1 dynamic-slice_bitcast_fusion.1
  177.2 0.9 copy.28
  (18 shorter events, 0.3 us)
Async XLA Ops:
  7.2 107.5 %reduce-scatter.2.cloned.1.call-start = ((), (), s32[]{:S(2)}) async-start(), calls=%async_computation.1 | async-start | bytes 5308416 | tf_op jit(solution)/shard_map/reduce_scatter | solution.py:312
  56.6 0.9 copy-start.1
  56.6 1.1 copy-start.2
  56.6 1.4 copy-start.3
  56.6 89.5 %all-gather.4.cloned.1.call-start = ((), (), s32[]{:S(2)}) async-start(), calls=%async_computation.2 | async-start | bytes 1474560 | tf_op jit(solution)/shard_map/all_gather | solution.py:316
  80.3 14.2 %collective-permute-start = (f32[2,32,8,128]{3,2,1,0:T(8,128)S(1)}, f32[2,32,8,128]{3,2,1,0:T(8,128)S(1)}, u32[]{:S(2)}, u32[]{:S(2)}) collective-permute-start(f32[2,32,8,128]{3,2,1,0:T(8,128)S(1)} %get-tuple-element.60), channel_id=1, source_target_pairs={{0,1},{1,2},{2,3},{3,4},{4,5},{5,6},{6,7},{8,9},{9,10},{10,11},{11... | collective-permute-start | bytes 786440 | tf_op jit(solution)/shard_map/ppermute | solution.py:256
  85.6 14.3 %collective-permute-start.1 = (f32[2,32,8,128]{3,2,1,0:T(8,128)S(1)}, f32[2,32,8,128]{3,2,1,0:T(8,128)S(1)}, u32[]{:S(2)}, u32[]{:S(2)}) collective-permute-start(f32[2,32,8,128]{3,2,1,0:T(8,128)S(1)} %get-tuple-element.61), channel_id=1, source_target_pairs={{1,0},{2,1},{3,2},{4,3},{5,4},{6,5},{7,6},{9,8},{10,9},{11,10},{12... | collective-permute-start | bytes 786440 | tf_op jit(solution)/shard_map/ppermute | solution.py:257
  149.1 13.1 %collective-permute-start.2 = (f32[6,32,8,128]{3,2,1,0:T(8,128)}, f32[6,32,8,128]{3,2,1,0:T(8,128)}, u32[]{:S(2)}, u32[]{:S(2)}) collective-permute-start(f32[6,32,8,128]{3,2,1,0:T(8,128)} %get-tuple-element.53), channel_id=1, source_target_pairs={{0,1},{1,2},{2,3},{3,4},{4,5},{5,6},{6,7},{8,9},{9,10},{10,11},{11... | collective-permute-start | bytes 2359304 | tf_op jit(solution)/shard_map/ppermute | solution.py:256
  152.9 13.6 %collective-permute-start.3 = (f32[6,32,8,128]{3,2,1,0:T(8,128)}, f32[6,32,8,128]{3,2,1,0:T(8,128)}, u32[]{:S(2)}, u32[]{:S(2)}) collective-permute-start(f32[6,32,8,128]{3,2,1,0:T(8,128)} %get-tuple-element.52), channel_id=1, source_target_pairs={{1,0},{2,1},{3,2},{4,3},{5,4},{6,5},{7,6},{9,8},{10,9},{11,10},{12... | collective-permute-start | bytes 2359304 | tf_op jit(solution)/shard_map/ppermute | solution.py:257
  174.3 2.8 %copy-start = (f32[32,16,128]{2,1,0:T(8,128)S(1)}, f32[32,16,128]{2,1,0:T(8,128)}, u32[]{:S(2)}) copy-start(f32[32,16,128]{2,1,0:T(8,128)} %get-tuple-element.24) | copy-start | bytes 786436
Sparse Core Ops, SparseCore 0:
  56.8 57.8 reduce-scatter.1
  118.4 27.7 all-gather.3
